TPU v7x, 32 devices: a whole 2x2x4 slice. The times are simulated.
32 devices in a mesh: groups: 2 (over y), tm: 4 (over z), space: 2 (over x), chan: 2 (over core).
Axes of the slice: x: 2, y: 2, z: 4, core: 2. Of those that a mesh axis runs over, the one named last changes fastest.
Arguments:
- activations: bfloat16 [256, 8, 16, 256], P(('groups', 'chan'), 'tm', 'space'), parts along dimension 0
- frame_clip: int32 [16], P(('groups', 'tm')), parts along dimension 0, may hold values from 0 to 3, as said below
- conv_weight: bfloat16 [3, 3, 3, 128, 128], replicated, may hold values from -0.109375 to 0.109375
- norm_gain: float32 [128], replicated, may hold values from 0.25 to 1.75
- norm_bias: float32 [128], replicated, may hold values from -3 to 3
- out_weight: bfloat16 [2, 2, 128, 32], replicated, may hold values from -0.25 to 0.25
- owner: int32 [4, 32, 1], P(('groups', 'space'), 'tm'), parts along dimension 0, may hold values from 0 to 3; in each aligned block of 8 rows (0 to 7, 8 to 15, ..., all dimensions but the last counted through in order) at most 4 rows name the same one
Outputs:
- owned: bfloat16 [4, 64, 32, 128], P(('groups', 'space'), 'tm', 'chan'), parts along dimension 0
There are 2 independent parts, one for each index of `groups`. A program takes and returns all parts, laid end to end along the dimension named above; an argument that names none is the same for every part. Nothing has to cross between parts.
Inputs may be any that keep to these rules, and one draw needn't show every extreme that they name: `frame_clip`: clip numbers never fall along the frames; each clip has 1 to 4 frames and one has exactly 4. Among the 8 rows of one tm index (aligned blocks), no owner is named more than 4 times; some owner is named exactly 4 times in some block.
All inputs are finite; a program needn't handle non-finite values.
Results may differ from a plain program's by a relative error of at most 0.012.
Values may be sent and summed in bfloat16 or wider, within the bound.
A program may use at most 64 MiB of HBM per device.

v0:
```python
import functools

import jax
import jax.numpy as jnp
from jax import lax
from jax.experimental import pallas as pl
from jax.experimental.pallas import tpu as pltpu
from jax.sharding import PartitionSpec as P

CHANNELS = 128
GROUPS = 32
GROUP_SIZE = CHANNELS // GROUPS
F32 = jnp.float32
BF16 = jnp.bfloat16
MESH = pl.DeviceIdType.MESH


def kernel(
    sizes, clip_hbm, owner_hbm, act_in, weight_in, gain_in, bias_in, out_weight_in, out,
    clip_in, owner_in, act_raw, act, weight, gain, bias, out_weight, meta_in,
    x, wt, conv, stat, stats, latent, arrived, meta, ids, sums,
    near_send, near_recv, zrow_send, zrow_recv, meta_send, meta_recv, stat_send, stat_recv,
    lat_send, lat_recv, extra_send, extra_recv, local_sem,
):
    n_tm, n_space, capacity, chunks = sizes
    frames_here, rows, half, columns = act.shape
    lanes = columns // 2
    total = n_tm * n_space * 2
    n_frames = n_tm * frames_here
    lat_rows = rows // 2
    step_rows = rows // chunks
    t = lax.axis_index("tm")
    s = lax.axis_index("space")
    c = lax.axis_index("chan")
    me = (t * n_space + s) * 2 + c
    first = t == 0
    piece_rows = lat_rows // 2
    reach = n_tm // 2
    has_main = jnp.logical_or(c == 1, t < n_tm - 1)

    def where_is(flat):
        return {"tm": flat // (2 * n_space), "space": (flat // 2) % n_space, "chan": flat % 2}

    fetches = [
        pltpu.make_async_copy(source, held, local_sem.at[1 + n])
        for n, (source, held) in enumerate((
            (act_in, act_raw), (weight_in, weight), (gain_in, gain), (bias_in, bias),
            (out_weight_in, out_weight),
            (clip_hbm, clip_in), (owner_hbm, owner_in),
        ))
    ]
    for fetch in fetches:
        fetch.start()
    stats[...] = jnp.zeros_like(stats)
    stat[...] = jnp.zeros_like(stat)

    barrier = pltpu.get_barrier_semaphore()

    @pl.loop(1, total)
    def _(step):
        pl.semaphore_signal(
            barrier, inc=1, device_id=where_is(lax.rem(me + step, total)), device_id_type=MESH
        )

    fetches[5].wait()
    fetches[6].wait()
    place = lax.broadcasted_iota(jnp.int32, (8, 128), 1)
    numbers = jnp.zeros((8, 128), jnp.int32)
    for n in range(frames_here):
        numbers = jnp.where(place == n, clip_in[0, n], numbers)
    for n in range(frames_here * lat_rows):
        numbers = jnp.where(place == frames_here + n, owner_in[0, n], numbers)
    meta_in[...] = numbers
    meta[t] = numbers
    fetches[0].wait()
    for f in range(frames_here):
        turned = jnp.transpose(act_raw[:, f], (1, 0, 2))
        act[f] = turned
        x[c + f, pl.ds(1, rows), c] = turned

    pl.semaphore_wait(barrier, total - 1)

    def remote(src, dst, send, recv, device):
        return pltpu.make_async_remote_copy(
            src_ref=src, dst_ref=dst, send_sem=send, recv_sem=recv, device_id=device,
            device_id_type=MESH,
        )

    def meta_copy(target):
        return remote(
            meta_in, meta.at[t], meta_send.at[target], meta_recv.at[t],
            {"tm": target, "space": s, "chan": c},
        )

    @pl.loop(1, n_tm)
    def _(step):
        meta_copy(lax.rem(t + step, n_tm)).start()

    up_ok, down_ok = t < n_tm - 1, t > 0
    t_up, t_down = jnp.minimum(t + 1, n_tm - 1), jnp.maximum(t - 1, 0)

    def zrow(up, piece):
        frame, slot, core, tt = (1, 0, 1, t_up) if up else (0, 2, 0, t_down)
        return remote(
            act.at[frame, pl.ds(piece * step_rows, step_rows)],
            x.at[slot, pl.ds(1 + piece * step_rows, step_rows), c],
            zrow_send.at[int(up), piece], zrow_recv.at[c, piece],
            {"tm": tt, "space": s, "chan": core},
        )

    def space_of(low):
        return jnp.maximum(s - 1, 0) if low else jnp.minimum(s + 1, n_space - 1)

    def edge(low, core):
        return remote(
            act.at[:, 0 if low else rows - 1],
            x.at[pl.ds(core, 2), rows + 1 if low else 0, c],
            near_send.at[int(low) * 2 + core], near_recv.at[int(low) * 2 + c],
            {"tm": t, "space": space_of(low), "chan": core},
        )

    def zedge(up, low):
        frame, slot, core, tt = (1, 0, 1, t_up) if up else (0, 2, 0, t_down)
        return remote(
            act.at[frame, 0 if low else rows - 1],
            x.at[slot, rows + 1 if low else 0, c],
            near_send.at[4 + int(low) * 2 + int(up)], near_recv.at[4 + int(low) * 2 + c],
            {"tm": tt, "space": space_of(low), "chan": core},
        )

    peer = remote(
        act, x.at[pl.ds(1 - c, 2), pl.ds(1, rows), c], near_send.at[8], near_recv.at[8],
        {"tm": t, "space": s, "chan": 1 - c},
    )
    low_ok, high_ok = s > 0, s < n_space - 1
    sides = ((True, low_ok), (False, high_ok))
    zs = ((True, up_ok), (False, down_ok))

    peer.start()
    for low, ok in sides:
        for up, z_ok in zs:
            @pl.when(jnp.logical_and(ok, z_ok))
            def _(low=low, up=up):
                zedge(up, low).start()
    for piece in range(chunks):
        for up, z_ok in zs:
            @pl.when(z_ok)
            def _(piece=piece, up=up):
                zrow(up, piece).start()
    for low, ok in sides:
        @pl.when(ok)
        def _(low=low):
            edge(low, 0).start()
            edge(low, 1).start()

    zero_row = jnp.zeros((3, 2, half, columns), BF16)

    @pl.when(s == 0)
    def _():
        x[:, 0] = zero_row

    @pl.when(s == n_space - 1)
    def _():
        x[:, rows + 1] = zero_row

    @pl.when(jnp.logical_and(first, c == 1))
    def _():
        x[0, pl.ds(1, rows)] = jnp.zeros((rows, 2, half, columns), BF16)

        @pl.when(s > 0)
        def _():
            x[0, 0] = zero_row[0]

        @pl.when(s < n_space - 1)
        def _():
            x[0, rows + 1] = zero_row[0]

    for fetch in fetches[1:5]:
        fetch.wait()
    for k in range(3):
        for i in range(3):
            for j in range(3):
                wt[k, pl.ds(j * 128, 128), pl.ds(i * 128, 128)] = weight[k, i, j].T
    gain_c = jnp.broadcast_to(gain[...], (128, 128)).T
    bias_c = jnp.broadcast_to(bias[...], (128, 128)).T * 0.5

    @pl.loop(1, n_tm)
    def _(step):
        source = lax.rem(t + step, n_tm)
        remote(
            meta_in, meta.at[source], meta_send.at[source], meta_recv.at[source],
            {"tm": source, "space": s, "chan": c},
        ).wait_recv()

    to_scalars = pltpu.make_async_copy(meta, ids, local_sem.at[0])
    to_scalars.start()
    to_scalars.wait()

    def clip_of(frame):
        frame = jnp.minimum(frame, n_frames - 1)
        return ids[frame // 2, 0, frame % 2]

    my_frame = 2 * t + 2 - c
    my_clip = clip_of(my_frame)
    older = jnp.logical_and(my_frame >= 2, clip_of(jnp.maximum(my_frame - 2, 0)) == my_clip)
    newer = clip_of(jnp.maximum(my_frame - 1, 0)) == my_clip

    peer.wait_recv()
    for low, ok in ((True, high_ok), (False, low_ok)):
        for core in range(2):
            @pl.when(ok)
            def _(low=low, core=core):
                remote(
                    act.at[:, 0], x.at[pl.ds(c, 2), rows + 1 if low else 0, core],
                    near_send.at[int(low) * 2 + core], near_recv.at[int(low) * 2 + core],
                    {"tm": t, "space": s, "chan": c},
                ).wait_recv()

    lane = lax.broadcasted_iota(jnp.int32, (CHANNELS, columns), 1)

    def conv_row(h, kept, taps):
        acc = None
        for k in range(3):
            term = jnp.dot(wt[k], taps[k](h), preferred_element_type=F32)
            acc = term if acc is None else acc + term
        left = jnp.where(lane == 0, 0.0, pltpu.roll(acc[0:128], 1, 1))
        right = jnp.where(lane == columns - 1, 0.0, pltpu.roll(acc[256:384], columns - 1, 1))
        value = (left + acc[128:256] + right).astype(BF16)
        conv[kept, h] = value
        value = value.astype(F32)
        a, b = value[:, :lanes], value[:, lanes:]
        sums[0] += a + b
        sums[1] += a * a + b * b

    def slab(slot):
        return lambda h: x[slot, pl.ds(h, 3)].reshape(3 * CHANNELS, columns)

    def sums_to(row):
        stat[pl.ds(row, 1), :] = jnp.sum(sums[0].T, axis=0, keepdims=True)
        stat[pl.ds(row + 1, 1), :] = jnp.sum(sums[1].T, axis=0, keepdims=True)

    @pl.when(first)
    def _():
        sums[...] = jnp.zeros_like(sums)

        @pl.loop(c * (rows // 2), (c + 1) * (rows // 2))
        def _(h):
            conv_row(h, 1, [slab(c)] * 3)

        sums_to(2)

    gets_z = jnp.logical_or(jnp.logical_and(c == 1, down_ok), jnp.logical_and(c == 0, up_ok))
    z_slot = 2 * (1 - c)

    def wait_zedge(low, ok):
        for core in range(2):
            @pl.when(jnp.logical_and(gets_z, ok))
            def _(core=core):
                remote(
                    act.at[0, 0], x.at[z_slot, rows + 1 if low else 0, core],
                    near_send.at[4 + int(low) * 2], near_recv.at[4 + int(low) * 2 + core],
                    {"tm": t, "space": s, "chan": c},
                ).wait_recv()

    def wait_zrow(piece):
        for core in range(2):
            @pl.when(gets_z)
            def _(core=core):
                remote(
                    act.at[0, pl.ds(piece * step_rows, step_rows)],
                    x.at[z_slot, pl.ds(1 + piece * step_rows, step_rows), core],
                    zrow_send.at[0, piece], zrow_recv.at[core, piece],
                    {"tm": t, "space": s, "chan": c},
                ).wait_recv()

    def tap_old(h):
        return jnp.where(older, slab(0)(h), tap_mid(h))

    def tap_mid(h):
        return jnp.where(newer, slab(1)(h), slab(2)(h))

    taps = [tap_old, tap_mid, slab(2)]
    wait_zedge(False, low_ok)
    wait_zedge(True, high_ok)

    @pl.when(has_main)
    def _():
        sums[...] = jnp.zeros_like(sums)

    for piece in range(chunks):
        wait_zrow(piece)
        begin = 0 if piece == 0 else piece * step_rows - 1
        end = rows if piece == chunks - 1 else (piece + 1) * step_rows - 1

        @pl.when(has_main)
        def _(begin=begin, end=end):
            @pl.loop(begin, end)
            def _(h):
                conv_row(h, 0, taps)

    @pl.when(has_main)
    def _():
        sums_to(0)

    def stat_copy(target):
        return remote(
            stat, stats.at[me], stat_send.at[target], stat_recv.at[me], where_is(target)
        )

    stats[me] = stat[...]

    def near(device):
        return jnp.abs(device // (2 * n_space) - t) <= reach

    @pl.loop(1, total)
    def _(step):
        target = lax.rem(me + step, total)

        @pl.when(near(target))
        def _():
            stat_copy(target).start()

    spread_row = lax.broadcasted_iota(jnp.int32, (columns, columns), 0)
    spread_col = lax.broadcasted_iota(jnp.int32, (columns, columns), 1)
    picked = jnp.where(spread_col < lanes, 2 * spread_col, 2 * (spread_col - lanes) + 1)
    spread = jnp.where(spread_row == picked, 1.0, 0.0).astype(BF16)

    @pl.loop(1, total)
    def _(step):
        source = lax.rem(me + step, total)

        @pl.when(near(source))
        def _():
            remote(
                stat, stats.at[source], stat_send.at[source], stat_recv.at[source],
                where_is(source),
            ).wait_recv()

    lane8 = lax.broadcasted_iota(jnp.int32, (8, 128), 1)

    def group_sum(v):
        v = v + jnp.where(lane8 % 2 == 0, pltpu.roll(v, 127, 1), pltpu.roll(v, 1, 1))
        return v + jnp.where(lane8 % 4 < 2, pltpu.roll(v, 126, 1), pltpu.roll(v, 2, 1))

    weights = jnp.concatenate([out_weight[q] for q in range(4)], axis=1)

    def moments_of(clip):
        def add_main(source, carry):
            frame = 2 * (source // (2 * n_space)) + 2 - source % 2
            same = jnp.logical_and(frame < n_frames, clip_of(frame) == clip)
            return carry + jnp.where(same, stats[source], 0.0)

        gathered = lax.fori_loop(0, total, add_main, jnp.zeros((8, 128), F32))
        zero_frame = jnp.zeros((8, 128), F32)
        for n in range(2 * n_space):
            zero_frame += stats[n]
        zero_frame = jnp.where(clip_of(0) == clip, zero_frame, 0.0)
        number = jnp.float32(0)
        for frame in range(n_frames):
            number += jnp.where(clip_of(frame) == clip, 1.0, 0.0)
        count = number * float(rows * n_space * columns * GROUP_SIZE)
        gathered = group_sum(gathered)
        zero_frame = group_sum(zero_frame)
        count = jnp.broadcast_to(count, (1, 128))
        mean = (gathered[0:1] + zero_frame[2:3]) / count
        var = (gathered[1:2] + zero_frame[3:4]) / count - mean * mean
        rstd = lax.rsqrt(var + 1e-6)
        mean_c = jnp.broadcast_to(mean, (128, 128)).T
        scale_c = jnp.broadcast_to(rstd, (128, 128)).T * gain_c * 0.5
        return mean_c, scale_c

    def finish(kept, piece, mean_c, scale_c):
        rows_in = []
        for q in range(2 * piece_rows):
            value = conv[kept, 2 * piece_rows * piece + q].astype(F32)
            pieces = []
            for u in range(2):
                v = (value[:, u * lanes:(u + 1) * lanes] - mean_c) * scale_c + bias_c
                pieces.append((v + v * jnp.tanh(v)).astype(BF16))
            rows_in.append(jnp.concatenate(pieces, axis=1))
        sorted_ = jnp.dot(
            jnp.concatenate(rows_in, axis=0), spread, preferred_element_type=F32
        ).astype(BF16)
        wide = jnp.concatenate(
            [
                jnp.concatenate(
                    [
                        sorted_[(2 * r + i) * 128:(2 * r + i + 1) * 128, j * lanes:(j + 1) * lanes]
                        for i in range(2) for j in range(2)
                    ],
                    axis=0,
                )
                for r in range(piece_rows)
            ],
            axis=1,
        )
        result = jnp.dot(weights, wide, preferred_element_type=F32).astype(BF16)
        for r in range(piece_rows):
            latent[kept, 0, piece * piece_rows + r] = result[0:16, r * lanes:(r + 1) * lanes]
            latent[kept, 1, piece * piece_rows + r] = result[16:32, r * lanes:(r + 1) * lanes]

    def lat_copy(kept, piece, frame, target, core, send, recv):
        span = pl.ds(piece * piece_rows, piece_rows)
        return remote(
            latent.at[kept, core, span], arrived.at[frame, span], send.at[target * 2 + core], recv,
            {"tm": target, "space": s, "chan": core},
        )

    here = t * 2 + c
    places = n_tm * 2

    def send_latent(kept, piece, frame, send, recv):
        span = pl.ds(piece * piece_rows, piece_rows)
        arrived[frame, span] = latent[kept, c, span]

        @pl.loop(1, places)
        def _(step):
            target = lax.rem(here + step, places)
            lat_copy(kept, piece, frame, target // 2, target % 2, send, recv).start()

    @pl.when(first)
    def _():
        finish(1, c, *moments_of(clip_of(0)))
        send_latent(1, c, 0, extra_send, extra_recv.at[c])

    @pl.when(has_main)
    def _():
        found = moments_of(my_clip)
        for piece in range(2):
            finish(0, piece, *found)
            send_latent(0, piece, my_frame, lat_send.at[piece], lat_recv.at[my_frame, piece])

    @pl.loop(1, n_frames)
    def _(frame):
        @pl.when(frame != my_frame)
        def _():
            for piece in range(2):
                lat_copy(
                    0, piece, frame, t, c, lat_send.at[piece], lat_recv.at[frame, piece]
                ).wait_recv()

    for piece in range(2):
        @pl.when(jnp.logical_not(jnp.logical_and(first, c == piece)))
        def _(piece=piece):
            lat_copy(0, piece, 0, t, c, lat_send.at[piece], extra_recv.at[piece]).wait_recv()

    @pl.loop(0, n_tm)
    def _(b):
        taken = jnp.int32(0)
        slots = []
        for n in range(2 * lat_rows):
            hit = ids[b, 0, frames_here + n] == t
            slots.append(jnp.where(hit, taken, -1))
            taken = taken + jnp.where(hit, 1, 0)
        for j in range(capacity):
            value = jnp.zeros((16, lanes), BF16)
            for n in range(2 * lat_rows):
                row = arrived[2 * b + n // lat_rows, n % lat_rows]
                value = jnp.where(slots[n] == j, row, value)
            out[0, b * capacity + j] = value

    @pl.loop(1, n_tm)
    def _(step):
        meta_copy(lax.rem(t + step, n_tm)).wait_send()

    peer.wait_send()
    for low, ok in sides:
        for up, z_ok in zs:
            @pl.when(jnp.logical_and(ok, z_ok))
            def _(low=low, up=up):
                zedge(up, low).wait_send()

        @pl.when(ok)
        def _(low=low):
            edge(low, 0).wait_send()
            edge(low, 1).wait_send()
    for piece in range(chunks):
        for up, z_ok in zs:
            @pl.when(z_ok)
            def _(piece=piece, up=up):
                zrow(up, piece).wait_send()

    @pl.loop(1, total)
    def _(step):
        target = lax.rem(me + step, total)

        @pl.when(near(target))
        def _():
            stat_copy(target).wait_send()

    def latents_left(kept, piece, frame, send, recv):
        @pl.loop(1, places)
        def _(step):
            target = lax.rem(here + step, places)
            lat_copy(kept, piece, frame, target // 2, target % 2, send, recv).wait_send()

    @pl.when(first)
    def _():
        latents_left(1, c, 0, extra_send, extra_recv.at[c])

    @pl.when(has_main)
    def _():
        for piece in range(2):
            latents_left(0, piece, my_frame, lat_send.at[piece], lat_recv.at[my_frame, piece])


def solution(mesh):
    n_tm, n_space = mesh.shape["tm"], mesh.shape["space"]
    total = n_tm * n_space * 2

    def shards(activations, frame_clip, conv_weight, norm_gain, norm_bias, out_weight, owner):
        half, frames_here, rows, columns = activations.shape
        lat_rows = rows // 2
        capacity = max(2, 2 * frames_here * lat_rows // n_tm)
        chunks = rows
        moments = out_weight.shape[-1]
        dma = pltpu.SemaphoreType.DMA
        return pl.pallas_call(
            functools.partial(kernel, (n_tm, n_space, capacity, chunks)),
            out_shape=jax.ShapeDtypeStruct(
                (1, n_tm * capacity, moments // 2, columns // 2), BF16
            ),
            in_specs=[pl.BlockSpec(memory_space=pltpu.HBM)] * 7,
            out_specs=pl.BlockSpec(memory_space=pltpu.VMEM),
            scratch_shapes=[
                pltpu.SMEM((1, frames_here), jnp.int32),
                pltpu.SMEM((1, frames_here * lat_rows), jnp.int32),
                pltpu.VMEM(activations.shape, BF16),
                pltpu.VMEM((frames_here, rows, half, columns), BF16),
                pltpu.VMEM(conv_weight.shape, BF16),
                pltpu.VMEM((1, CHANNELS), F32),
                pltpu.VMEM((1, CHANNELS), F32),
                pltpu.VMEM((4, moments, CHANNELS), BF16),
                pltpu.VMEM((8, 128), jnp.int32),
                pltpu.VMEM((3, rows + 2, 2, half, columns), BF16),
                pltpu.VMEM((3, 384, 384), BF16),
                pltpu.VMEM((2, rows, CHANNELS, columns), BF16),
                pltpu.VMEM((8, 128), F32),
                pltpu.VMEM((total, 8, 128), F32),
                pltpu.VMEM((2, 2, lat_rows, moments // 2, columns // 2), BF16),
                pltpu.VMEM((n_tm * frames_here, lat_rows, moments // 2, columns // 2), BF16),
                pltpu.VMEM((n_tm, 8, 128), jnp.int32),
                pltpu.SMEM((n_tm, 8, 128), jnp.int32),
                pltpu.VMEM((2, CHANNELS, columns // 2), F32),
                dma((9,)),
                dma((9,)),
                dma((2, chunks)),
                dma((2, chunks)),
                dma((n_tm,)),
                dma((n_tm,)),
                dma((total,)),
                dma((total,)),
                dma((2, 2 * n_tm)),
                dma((n_tm * frames_here, 2)),
                dma((2 * n_tm,)),
                dma((2,)),
                dma((8,)),
            ],
            compiler_params=pltpu.CompilerParams(
                collective_id=0, has_side_effects=True, vmem_limit_bytes=67_043_328
            ),
        )(
            frame_clip.reshape(1, -1), owner.reshape(1, -1), activations, conv_weight,
            norm_gain.reshape(1, -1), norm_bias.reshape(1, -1),
            out_weight.transpose(0, 1, 3, 2).reshape(4, moments, CHANNELS),
        )

    placed = (
        P(("groups", "chan"), "tm", "space", None),
        P(("groups", "tm")),
        P(),
        P(),
        P(),
        P(),
        P(("groups", "space"), "tm", None),
    )
    return jax.shard_map(
        shards,
        mesh=mesh,
        in_specs=placed,
        out_specs=P(("groups", "space"), "tm", "chan", None),
        check_vma=False,
    )
```

profile of v0, /device:TPU:0, one launch (start us, length us, event | category | flops | bytes accessed | tf_op | source)
XLA Modules:
  0.0 30.6 jit_solution(8501523618342789290)
XLA Ops:
  0.0 29.2 %shard_map.73 = bf16[1,16,16,128]{3,2,1,0:T(8,128)(2,1)} custom-call(s32[1,2]{1,0:T(1,128)} %bitcast.8, s32[1,8]{1,0:T(1,128)} %bitcast.9, bf16[64,2,8,256]{3,2,1,0:T(8,128)(2,1)} %act_in.1, bf16[3,3,3,128,128]{4,3,2,1,0:T(8,128)(2,1)} %weight_in.1, f32[1,128]{1,0:T(1,128)} %bitcast.10, f32[1,128]{1,0:T(1,128)} %bitcast.11, bf16[4,32,128]{2,1,0:T(8,128)(2,1)} %bitcast.7), custom_call_target="tpu_custom_call" | custom-call | tf_op jit(solution)/shard_map/pallas_call | solution.py:518
  29.2 1.5 %copy.9 = bf16[1,16,16,128]{3,2,1,0:T(8,128)(2,1)} copy(bf16[1,16,16,128]{3,2,1,0:T(8,128)(2,1)} %shard_map.73) | data formatting | bytes 131072
where the time goes:
time: 30.8 us; the launch traced here: 30.6 us
  Pallas kernels  29.2 us (95%)
  local copies, waits for them, and re-layouts  1.47 us (5%)
    pallas_call x1, Pallas kernels, shards(): pl.pallas_call(functools.partial(kernel, (n_tm, n_space, capacity, chunks...  29.2 us
    unnamed x1, local copies, waits for them, and re-layouts  1.47 us

commit v1 on v0

--- a/solution.py
+++ b/solution.py
@@ -557,13 +557,16 @@
                 dma((8,)),
             ],
             compiler_params=pltpu.CompilerParams(
-                collective_id=0, has_side_effects=True, vmem_limit_bytes=67_043_328
+                collective_id=0, has_side_effects=True, vmem_limit_bytes=24 * 1024 * 1024
             ),
-        )(
-            frame_clip.reshape(1, -1), owner.reshape(1, -1), activations, conv_weight,
-            norm_gain.reshape(1, -1), norm_bias.reshape(1, -1),
-            out_weight.transpose(0, 1, 3, 2).reshape(4, moments, CHANNELS),
-        )
+        )(*(
+            pltpu.with_memory_space_constraint(operand, pltpu.HBM)
+            for operand in (
+                frame_clip.reshape(1, -1), owner.reshape(1, -1), activations, conv_weight,
+                norm_gain.reshape(1, -1), norm_bias.reshape(1, -1),
+                out_weight.transpose(0, 1, 3, 2).reshape(4, moments, CHANNELS),
+            )
+        ))
 
     placed = (
         P(("groups", "chan"), "tm", "space", None),

time: 30.8 us -> 29.3 us (0.951)
  local copies, waits for them, and re-layouts: 1.47 us -> 0.63 us
  Pallas kernels: 29.2 us -> 28.5 us
    unnamed x1, local copies, waits for them, and re-layouts: 1.47 us -> 0.63 us
    pallas_call x1, Pallas kernels: 29.2 us -> 28.5 us  [shards(): pl.pallas_call(functools.partial(kernel, (n_tm, n_space, capacity, chunks...]
where the time goes in v1:
time: 29.3 us; the launch traced here: 29.2 us
  Pallas kernels  28.5 us (97%)
  local copies, waits for them, and re-layouts  0.63 us (2%)
    pallas_call x1, Pallas kernels, shards(): pl.pallas_call(functools.partial(kernel, (n_tm, n_space, capacity, chunks...  28.5 us
    unnamed x1, local copies, waits for them, and re-layouts  0.63 us

profile of v1, /device:TPU:0, one launch (start us, length us, event | category | flops | bytes accessed | tf_op | source)
XLA Modules:
  0.0 29.2 jit_solution(6436859420658219189)
XLA Ops:
  0.0 28.5 %shard_map.73 = bf16[1,16,16,128]{3,2,1,0:T(8,128)(2,1)S(1)} custom-call(s32[1,2]{1,0:T(1,128)} %bitcast.8, s32[1,8]{1,0:T(1,128)} %bitcast.9, bf16[64,2,8,256]{3,2,1,0:T(8,128)(2,1)} %act_in.1, bf16[3,3,3,128,128]{4,3,2,1,0:T(8,128)(2,1)} %weight_in.1, f32[1,128]{1,0:T(1,128)} %bitcast.10, f32[1,128]{1,0:T(1,128)} %bitcast.11, bf16[4,32,128]{2,1,0:T(8,128)(2,1)} %bitcast.7), custom_call_target="tpu_custom_call" | custom-call | tf_op jit(solution)/shard_map/pallas_call | solution.py:518
  28.6 0.6 %copy.9 = bf16[1,16,16,128]{3,2,1,0:T(8,128)(2,1)} copy(bf16[1,16,16,128]{3,2,1,0:T(8,128)(2,1)S(1)} %shard_map.73) | data formatting | bytes 131072

commit v2 on v1

v2 whole, which is shorter than its diff:
```python
import functools

import jax
import jax.numpy as jnp
from jax import lax
from jax.experimental import pallas as pl
from jax.experimental.pallas import tpu as pltpu
from jax.sharding import PartitionSpec as P

CHANNELS = 128
GROUPS = 32
GROUP_SIZE = CHANNELS // GROUPS
F32 = jnp.float32
BF16 = jnp.bfloat16
MESH = pl.DeviceIdType.MESH


def kernel(
    sizes, clip_hbm, owner_hbm, act_in, weight_in, gain_in, bias_in, out_weight_in, out,
    clip_in, owner_in, act_raw, weight, gain, bias, out_weight, meta_in, near_meta, near_ids,
    x, wt, conv, stat, stats, ids, latent, arrived, sums,
    round_sem, z_send, z_recv, edge_send, edge_recv, fwd_send, fwd_recv, peer_send, peer_recv,
    meta_send, meta_recv, stat_send, stat_recv, lat_send, lat_recv, local_sem,
):
    n_tm, n_space, capacity = sizes
    half, frames_here, rows, columns = act_raw.shape
    lanes = columns // 2
    total = n_tm * n_space * 2
    n_frames = n_tm * frames_here
    lat_rows = rows // 2
    own_rows = frames_here * lat_rows
    piece_rows = lat_rows // 2
    half_rows = rows // 2
    t = lax.axis_index("tm")
    s = lax.axis_index("space")
    c = lax.axis_index("chan")
    me = (t * n_space + s) * 2 + c
    first = t == 0
    has_main = jnp.logical_or(c == 1, t < n_tm - 1)
    mirror = n_space == 2
    flip = s == 0 if mirror else False
    rounds = max(n_tm // 2 + n_space - 1, n_tm - 1) - 1

    def row_of(p):
        return jnp.where(flip, rows - 1 - p, p) if mirror else p

    fetches = [
        pltpu.make_async_copy(source, held, local_sem.at[n])
        for n, (source, held) in enumerate((
            (act_in, act_raw), (clip_hbm, clip_in), (owner_hbm, owner_in), (weight_in, weight),
            (gain_in, gain), (bias_in, bias), (out_weight_in, out_weight),
        ))
    ]
    for fetch in fetches:
        fetch.start()
    stats[...] = jnp.full(stats.shape, -1.0, F32)

    up_ok, down_ok = t < n_tm - 1, t > 0
    low_ok, high_ok = s > 0, s < n_space - 1
    t_up, t_down = jnp.minimum(t + 1, n_tm - 1), jnp.maximum(t - 1, 0)
    s_low, s_high = jnp.maximum(s - 1, 0), jnp.minimum(s + 1, n_space - 1)
    around = [(up_ok, t_up, s), (down_ok, t_down, s), (low_ok, t, s_low), (high_ok, t, s_high)]
    near_count = jnp.int32(1)
    for ok, _, _ in around:
        near_count = near_count + jnp.where(ok, 2, 0)

    def greet(semaphore):
        for ok, tt, ss in around:
            @pl.when(ok)
            def _(tt=tt, ss=ss):
                for core in range(2):
                    pl.semaphore_signal(
                        semaphore, inc=1, device_id={"tm": tt, "space": ss, "chan": core},
                        device_id_type=MESH,
                    )
        pl.semaphore_signal(
            semaphore, inc=1, device_id={"tm": t, "space": s, "chan": 1 - c}, device_id_type=MESH
        )

    barrier = pltpu.get_barrier_semaphore()
    greet(barrier)

    zero_row = jnp.zeros((3, 2, half, columns), BF16)

    @pl.when(s == 0)
    def _():
        x[:, 0] = zero_row

    @pl.when(s == n_space - 1)
    def _():
        x[:, rows + 1] = zero_row

    fetches[1].wait()
    fetches[2].wait()
    place = lax.broadcasted_iota(jnp.int32, (8, 128), 1)
    numbers = jnp.zeros((8, 128), jnp.int32)
    for n in range(frames_here):
        numbers = jnp.where(place == n, clip_in[0, n], numbers)
    meta_in[...] = numbers

    @pl.when(first)
    def _():
        near_meta[0] = numbers

    @pl.when(t == n_tm - 1)
    def _():
        near_meta[1] = numbers

    fetches[0].wait()
    for f in range(frames_here):
        x[c + f, pl.ds(1, rows), c] = jnp.transpose(act_raw[:, f], (1, 0, 2))

    pl.semaphore_wait(barrier, near_count)

    def remote(src, dst, send, recv, device):
        return pltpu.make_async_remote_copy(
            src_ref=src, dst_ref=dst, send_sem=send, recv_sem=recv, device_id=device,
            device_id_type=MESH,
        )

    def z_copy(up, p, count):
        frame, slot, core, tt = (1, 0, 1, t_up) if up else (0, 2, 0, t_down)
        begin = 1 + (jnp.where(flip, rows - p - count, p) if mirror else p)
        return remote(
            x.at[c + frame, pl.ds(begin, count), c], x.at[slot, pl.ds(begin, count), c],
            z_send.at[int(up)], z_recv.at[p], {"tm": tt, "space": s, "chan": core},
        )

    def meta_copy(up):
        return remote(
            meta_in, near_meta.at[0 if up else 1], meta_send.at[int(up)],
            meta_recv.at[0 if up else 1],
            {"tm": t_up if up else t_down, "space": s, "chan": c},
        )

    def edge(low, core):
        return remote(
            x.at[pl.ds(c, 2), 1 if low else rows, c],
            x.at[pl.ds(core, 2), rows + 1 if low else 0, c],
            edge_send.at[int(low)], edge_recv.at[int(low)],
            {"tm": t, "space": s_low if low else s_high, "chan": core},
        )

    z_slot = 2 * (1 - c)

    def forward(low):
        return remote(
            x.at[z_slot, 1 if low else rows], x.at[z_slot, rows + 1 if low else 0],
            fwd_send.at[int(low)], fwd_recv.at[int(low)],
            {"tm": t, "space": s_low if low else s_high, "chan": c},
        )

    peer = remote(
        x.at[pl.ds(c, 2), pl.ds(1, rows), c], x.at[pl.ds(1 - c, 2), pl.ds(1, rows), c],
        peer_send.at[0], peer_recv.at[0], {"tm": t, "space": s, "chan": 1 - c},
    )
    zs = ((True, up_ok), (False, down_ok))
    sides = ((True, low_ok), (False, high_ok))

    for p in range(2):
        for up, ok in zs:
            @pl.when(ok)
            def _(up=up, p=p):
                z_copy(up, p, 1).start()
    peer.start()
    for low, ok in sides:
        @pl.when(ok)
        def _(low=low):
            edge(low, 0).start()
            edge(low, 1).start()
    for up, ok in zs:
        @pl.when(ok)
        def _(up=up):
            meta_copy(up).start()
    for p in range(2, rows):
        for up, ok in zs:
            @pl.when(ok)
            def _(up=up, p=p):
                z_copy(up, p, 1).start()
    if rounds > 0:
        greet(round_sem.at[0])

    fetches[3].wait()
    for k in range(3):
        for i in range(3):
            for j in range(3):
                wt[k, pl.ds(j * 128, 128), pl.ds(i * 128, 128)] = weight[k, i, j].T
    for fetch in fetches[4:]:
        fetch.wait()

    for up, ok in zs:
        @pl.when(ok)
        def _(up=up):
            meta_copy(not up).wait_recv()
    to_scalars = pltpu.make_async_copy(near_meta, near_ids, local_sem.at[7])
    to_scalars.start()
    to_scalars.wait()

    my_clip = jnp.where(c == 1, clip_in[0, 1], near_ids[1, 0, 0])
    newer = jnp.where(c == 1, clip_in[0, 0], clip_in[0, 1]) == my_clip
    older = jnp.logical_and(
        jnp.logical_or(c == 0, t > 0),
        jnp.where(c == 1, near_ids[0, 0, 1], clip_in[0, 0]) == my_clip,
    )

    peer.wait_recv()
    if rounds > 0:
        pl.semaphore_wait(round_sem.at[0], near_count)

        @pl.loop(1, rounds)
        def _(r):
            greet(round_sem.at[lax.rem(r, 2)])

            @pl.when(r < rounds - 1)
            def _():
                pl.semaphore_wait(round_sem.at[lax.rem(r, 2)], near_count)

    lane = lax.broadcasted_iota(jnp.int32, (CHANNELS, columns), 1)

    def conv_row(h, kept, taps):
        acc = None
        for k in range(3):
            term = jnp.dot(wt[k], taps[k](h), preferred_element_type=F32)
            acc = term if acc is None else acc + term
        left = jnp.where(lane == 0, 0.0, pltpu.roll(acc[0:128], 1, 1))
        right = jnp.where(lane == columns - 1, 0.0, pltpu.roll(acc[256:384], columns - 1, 1))
        value = (left + acc[128:256] + right).astype(BF16)
        conv[kept, h] = value
        value = value.astype(F32)
        a, b = value[:, :lanes], value[:, lanes:]
        sums[0] += a + b
        sums[1] += a * a + b * b

    def slab(slot):
        return lambda h: x[slot, pl.ds(h, 3)].reshape(3 * CHANNELS, columns)

    def sums_to(row):
        stat[pl.ds(row, 1), :] = jnp.sum(sums[0].T, axis=0, keepdims=True)
        stat[pl.ds(row + 1, 1), :] = jnp.sum(sums[1].T, axis=0, keepdims=True)

    def wait_edges():
        for low, ok in ((True, high_ok), (False, low_ok)):
            @pl.when(ok)
            def _(low=low):
                there = x.at[pl.ds(c, 2), rows + 1 if low else 0]
                remote(
                    there, there, edge_send.at[int(low)], edge_recv.at[int(low)],
                    {"tm": t, "space": s, "chan": c},
                ).wait_recv()

    gets_z = jnp.logical_or(jnp.logical_and(c == 1, down_ok), jnp.logical_and(c == 0, up_ok))

    def wait_z(p):
        @pl.when(gets_z)
        def _():
            there = x.at[z_slot, pl.ds(1 + row_of(p), 1)]
            remote(
                there, there, z_send.at[0], z_recv.at[p], {"tm": t, "space": s, "chan": c}
            ).wait_recv()

    def start_forwards():
        for low, ok in sides:
            @pl.when(jnp.logical_and(gets_z, ok))
            def _(low=low):
                forward(low).start()

    def wait_forwards():
        for low, ok in ((True, high_ok), (False, low_ok)):
            @pl.when(jnp.logical_and(gets_z, ok))
            def _(low=low):
                forward(low).wait_recv()

    row8 = lax.broadcasted_iota(jnp.int32, (8, 128), 0)
    lane8 = lax.broadcasted_iota(jnp.int32, (8, 128), 1)
    facts = jnp.where(row8 == 2, jnp.where(has_main, my_clip, -1).astype(F32), -1.0)
    facts = jnp.where(
        jnp.logical_and(row8 == 5, first), clip_in[0, 0].astype(F32), facts
    )
    for n in range(own_rows):
        facts = jnp.where(
            jnp.logical_and(row8 == 6, lane8 == n), owner_in[0, n].astype(F32), facts
        )
    stat[...] = facts

    half_index = jnp.where(flip, c, 1 - c) if mirror else c

    if not mirror:
        wait_edges()

    @pl.when(first)
    def _():
        sums[...] = jnp.zeros_like(sums)

        @pl.loop(0, half_rows)
        def _(n):
            if mirror:
                @pl.when(jnp.logical_and(c == 1, n == half_rows - 1))
                def _():
                    wait_edges()
            p = half_rows - 1 - n + jnp.where(c == 0, half_rows, 0) if mirror else (
                n + c * half_rows
            )
            conv_row(row_of(p), 1, [slab(c)] * 3)

        sums_to(3)

    def tap_old(h):
        return jnp.where(older, slab(0)(h), tap_mid(h))

    def tap_mid(h):
        return jnp.where(newer, slab(1)(h), slab(2)(h))

    taps = [tap_old, tap_mid, slab(2)]
    border_step = rows - 4

    if mirror:
        wait_z(0)
        start_forwards()
        wait_z(1)
    else:
        for p in range(rows):
            wait_z(p)
        start_forwards()
        wait_forwards()

    sums[...] = jnp.zeros_like(sums)

    @pl.loop(0, rows)
    def _(n):
        if mirror:
            @pl.when(n < border_step)
            def _():
                wait_z(n + 2)

            @pl.when(n == border_step)
            def _():
                @pl.when(jnp.logical_not(jnp.logical_and(first, c == 1)))
                def _():
                    wait_edges()
                wait_forwards()

            @pl.when(jnp.logical_and(n > border_step, n < rows - 1))
            def _():
                wait_z(n + 1)

            p = jnp.where(n < border_step, n + 1, jnp.where(n == border_step, 0, n))
        else:
            p = n

        @pl.when(has_main)
        def _():
            conv_row(row_of(p), 0, taps)

    @pl.when(has_main)
    def _():
        sums_to(0)

    if rounds > 1:
        pl.semaphore_wait(round_sem.at[(rounds - 1) % 2], near_count)

    stats[me] = stat[...]

    def needs(tt, ss, core):
        apart = jnp.abs(2 * (tt - t) + c - core) <= n_tm - 1
        return jnp.logical_or(apart, jnp.logical_and(ss == s, core == c))

    def stat_copy(tt, ss, core):
        target = (tt * n_space + ss) * 2 + core
        return remote(
            stat, stats.at[me], stat_send.at[target], stat_recv.at[me],
            {"tm": tt, "space": ss, "chan": core},
        )

    def stat_from(tt, ss, core):
        source = (tt * n_space + ss) * 2 + core
        return remote(
            stat, stats.at[source], stat_send.at[source], stat_recv.at[source],
            {"tm": tt, "space": ss, "chan": core},
        )

    def each_stat(act):
        @pl.loop(0, n_tm)
        def _(step):
            far = n_tm - 1 - step
            for up in (True, False):
                tt = t + far if up else t - far
                ok = jnp.logical_and(tt < n_tm, tt >= 0)
                if not up:
                    ok = jnp.logical_and(ok, far > 0)
                for ss in range(n_space):
                    for core in range(2):
                        use = jnp.logical_and(ok, needs(tt, ss, core))
                        other = (tt * n_space + ss) * 2 + core != me

                        @pl.when(jnp.logical_and(use, other))
                        def _(tt=tt, ss=ss, core=core):
                            act(tt, ss, core)

    each_stat(lambda tt, ss, core: stat_copy(tt, ss, core).start())

    spread_row = lax.broadcasted_iota(jnp.int32, (columns, lanes), 0)
    spread_col = lax.broadcasted_iota(jnp.int32, (columns, lanes), 1)
    spread = jnp.where(spread_row == 2 * spread_col, 1.0, 0.0).astype(BF16)
    weights = jnp.concatenate(
        [
            jnp.concatenate([out_weight[2 * i + j] for i in range(2)], axis=1)
            for j in range(2)
        ],
        axis=0,
    )

    each_stat(lambda tt, ss, core: stat_from(tt, ss, core).wait_recv())

    owners = [
        pltpu.make_async_copy(stats.at[(b * n_space + s) * 2 + c], ids.at[b], local_sem.at[8])
        for b in range(n_tm)
    ]
    for copy in owners:
        copy.start()

    sizes_row = jnp.where(
        row8 == 2, float(rows * columns), float(half_rows * columns)
    )
    is_size = jnp.logical_or(row8 == 2, row8 == 5)

    def add_source(source, carry, clip):
        value = stats[source]
        key = jnp.where(row8 < 3, value[2:3], value[5:6])
        value = jnp.where(is_size, sizes_row, value)
        return carry + jnp.where(key == clip, value, 0.0)

    def moments_of(clip):
        clip = clip.astype(F32)
        found = jnp.zeros((8, 128), F32)
        if total <= 32:
            for source in range(total):
                found = add_source(source, found, clip)
        else:
            found = lax.fori_loop(
                0, total, lambda source, carry: add_source(source, carry, clip), found
            )
        found = found + pltpu.roll(found, 5, 0)
        found = found + jnp.where(
            lane8 % 2 == 0, pltpu.roll(found, 127, 1), pltpu.roll(found, 1, 1)
        )
        found = found + jnp.where(
            lane8 % 4 < 2, pltpu.roll(found, 126, 1), pltpu.roll(found, 2, 1)
        )
        count = found[2:3]
        mean = found[0:1] / count
        var = found[1:2] / count - mean * mean
        scale = lax.rsqrt(var + 1e-6) * gain[...] * 0.5
        shift = bias[...] * 0.5 - mean * scale
        return jnp.broadcast_to(scale, (128, 128)).T, jnp.broadcast_to(shift, (128, 128)).T

    def finish(kept, begin, scale_c, shift_c):
        packed = []
        for r in range(piece_rows):
            pair = []
            for i in range(2):
                value = conv[kept, 2 * (begin + r) + i].astype(F32)
                pieces = []
                for u in range(2):
                    v = value[:, u * lanes:(u + 1) * lanes] * scale_c + shift_c
                    pieces.append((v + v * jnp.tanh(v)).astype(BF16))
                pair.append(jnp.concatenate(pieces, axis=1))
            both = jnp.dot(
                weights, jnp.concatenate(pair, axis=0), preferred_element_type=F32
            )
            packed.append((both[0:32] + pltpu.roll(both[32:64], columns - 1, 1)).astype(BF16))
        result = jnp.dot(
            jnp.concatenate(packed, axis=0), spread, preferred_element_type=F32
        ).astype(BF16)
        for r in range(piece_rows):
            for core in range(2):
                latent[kept, core, begin + r] = result[r * 32 + core * 16:r * 32 + core * 16 + 16]

    def send_latent(kept, begin, frame):
        span = pl.ds(frame * lat_rows + begin, piece_rows)
        arrived[span] = latent[kept, c, pl.ds(begin, piece_rows)]

        @pl.loop(0, n_tm)
        def _(step):
            far = n_tm - 1 - step
            for up in (True, False):
                tt = t + far if up else t - far
                ok = jnp.logical_and(tt < n_tm, tt >= 0)
                if not up:
                    ok = jnp.logical_and(ok, far > 0)
                for core in range(2):
                    other = jnp.logical_or(tt != t, core != c)

                    @pl.when(jnp.logical_and(ok, other))
                    def _(tt=tt, core=core):
                        remote(
                            latent.at[kept, core, pl.ds(begin, piece_rows)], arrived.at[span],
                            lat_send.at[kept], lat_recv.at[0],
                            {"tm": tt, "space": s, "chan": core},
                        ).start()

    my_frame = 2 * t + 2 - c

    @pl.when(first)
    def _():
        finish(1, half_index * piece_rows, *moments_of(clip_in[0, 0]))
        send_latent(1, half_index * piece_rows, 0)

    @pl.when(has_main)
    def _():
        found = moments_of(my_clip)
        for piece in range(2):
            finish(0, piece * piece_rows, *found)
            send_latent(0, piece * piece_rows, my_frame)

    pltpu.make_async_copy(stats.at[pl.ds(0, n_tm)], ids, local_sem.at[8]).wait()

    def arrived_wait(count):
        span = arrived.at[pl.ds(0, count)]
        remote(
            span, span, lat_send.at[0], lat_recv.at[0], {"tm": t, "space": s, "chan": c}
        ).wait_recv()

    every = n_frames * lat_rows

    @pl.when(first)
    def _():
        arrived_wait(every - lat_rows - piece_rows)

    @pl.when(jnp.logical_and(has_main, t > 0))
    def _():
        arrived_wait(every - lat_rows)

    @pl.when(jnp.logical_not(has_main))
    def _():
        arrived_wait(every)

    here = t.astype(F32)

    @pl.loop(0, n_tm)
    def _(b):
        taken = jnp.int32(0)
        slots = []
        for n in range(own_rows):
            hit = ids[b, 6, n] == here
            slots.append(jnp.where(hit, taken, -1))
            taken = taken + jnp.where(hit, 1, 0)
        for j in range(capacity):
            value = jnp.zeros((16, lanes), BF16)
            for n in range(own_rows):
                value = jnp.where(slots[n] == j, arrived[b * own_rows + n], value)
            out[0, b * capacity + j] = value

    peer.wait_send()
    for up, ok in zs:
        @pl.when(ok)
        def _(up=up):
            z_copy(up, 0, rows).wait_send()
            meta_copy(up).wait_send()
    for low, ok in sides:
        @pl.when(ok)
        def _(low=low):
            there = x.at[pl.ds(0, 2), 0]
            remote(
                there, there, edge_send.at[int(low)], edge_recv.at[int(low)],
                {"tm": t, "space": s, "chan": c},
            ).wait_send()

            @pl.when(gets_z)
            def _():
                forward(low).wait_send()

    each_stat(lambda tt, ss, core: stat_copy(tt, ss, core).wait_send())

    def latents_left(kept, count):
        span = arrived.at[pl.ds(0, count)]
        remote(
            span, span, lat_send.at[kept], lat_recv.at[0], {"tm": t, "space": s, "chan": c}
        ).wait_send()

    @pl.when(first)
    def _():
        latents_left(1, (2 * n_tm - 1) * piece_rows)

    @pl.when(has_main)
    def _():
        latents_left(0, (2 * n_tm - 1) * lat_rows)


def solution(mesh):
    n_tm, n_space = mesh.shape["tm"], mesh.shape["space"]
    total = n_tm * n_space * 2

    def shards(activations, frame_clip, conv_weight, norm_gain, norm_bias, out_weight, owner):
        half, frames_here, rows, columns = activations.shape
        lat_rows = rows // 2
        capacity = max(2, 2 * frames_here * lat_rows // n_tm)
        moments = out_weight.shape[-1]
        dma = pltpu.SemaphoreType.DMA
        return pl.pallas_call(
            functools.partial(kernel, (n_tm, n_space, capacity)),
            out_shape=jax.ShapeDtypeStruct(
                (1, n_tm * capacity, moments // 2, columns // 2), BF16
            ),
            in_specs=[pl.BlockSpec(memory_space=pltpu.HBM)] * 7,
            out_specs=pl.BlockSpec(memory_space=pltpu.VMEM),
            scratch_shapes=[
                pltpu.SMEM((1, frames_here), jnp.int32),
                pltpu.SMEM((1, frames_here * lat_rows), jnp.int32),
                pltpu.VMEM(activations.shape, BF16),
                pltpu.VMEM(conv_weight.shape, BF16),
                pltpu.VMEM((1, CHANNELS), F32),
                pltpu.VMEM((1, CHANNELS), F32),
                pltpu.VMEM((4, moments, CHANNELS), BF16),
                pltpu.VMEM((8, 128), jnp.int32),
                pltpu.VMEM((2, 8, 128), jnp.int32),
                pltpu.SMEM((2, 8, 128), jnp.int32),
                pltpu.VMEM((3, rows + 2, 2, half, columns), BF16),
                pltpu.VMEM((3, 384, 384), BF16),
                pltpu.VMEM((2, rows, CHANNELS, columns), BF16),
                pltpu.VMEM((8, 128), F32),
                pltpu.VMEM((total, 8, 128), F32),
                pltpu.SMEM((n_tm, 8, 128), F32),
                pltpu.VMEM((2, 2, lat_rows, moments // 2, columns // 2), BF16),
                pltpu.VMEM((n_tm * frames_here * lat_rows, moments // 2, columns // 2), BF16),
                pltpu.VMEM((2, CHANNELS, columns // 2), F32),
                pltpu.SemaphoreType.REGULAR((2,)),
                dma((2,)),
                dma((rows,)),
                dma((2,)),
                dma((2,)),
                dma((2,)),
                dma((2,)),
                dma((1,)),
                dma((1,)),
                dma((2,)),
                dma((2,)),
                dma((total,)),
                dma((total,)),
                dma((2,)),
                dma((1,)),
                dma((9,)),
            ],
            compiler_params=pltpu.CompilerParams(
                collective_id=0, has_side_effects=True, vmem_limit_bytes=24 * 1024 * 1024
            ),
        )(*(
            pltpu.with_memory_space_constraint(operand, pltpu.HBM)
            for operand in (
                frame_clip.reshape(1, -1), owner.reshape(1, -1), activations, conv_weight,
                norm_gain.reshape(1, -1), norm_bias.reshape(1, -1),
                out_weight.transpose(0, 1, 3, 2).reshape(4, moments, CHANNELS),
            )
        ))

    placed = (
        P(("groups", "chan"), "tm", "space", None),
        P(("groups", "tm")),
        P(),
        P(),
        P(),
        P(),
        P(("groups", "space"), "tm", None),
    )
    return jax.shard_map(
        shards,
        mesh=mesh,
        in_specs=placed,
        out_specs=P(("groups", "space"), "tm", "chan", None),
        check_vma=False,
    )
```

time: 29.3 us -> 26.4 us (0.901)
  Pallas kernels: 28.5 us -> 25.6 us
    pallas_call x1, Pallas kernels: 28.5 us -> 25.6 us  [shards(): pl.pallas_call(functools.partial(kernel, (n_tm, n_space, capacity)), out_...]
where the time goes in v2:
time: 26.4 us; the launch traced here: 26.2 us
  Pallas kernels  25.6 us (97%)
  local copies, waits for them, and re-layouts  0.63 us (2%)
    pallas_call x1, Pallas kernels, shards(): pl.pallas_call(functools.partial(kernel, (n_tm, n_space, capacity)), out_...  25.6 us
    unnamed x1, local copies, waits for them, and re-layouts  0.63 us

profile of v2, /device:TPU:0, one launch (start us, length us, event | category | flops | bytes accessed | tf_op | source)
XLA Modules:
  0.0 26.2 jit_solution(12593371967388539463)
XLA Ops:
  0.0 25.6 %shard_map.73 = bf16[1,16,16,128]{3,2,1,0:T(8,128)(2,1)S(1)} custom-call(s32[1,2]{1,0:T(1,128)} %bitcast.8, s32[1,8]{1,0:T(1,128)} %bitcast.9, bf16[64,2,8,256]{3,2,1,0:T(8,128)(2,1)} %act_in.1, bf16[3,3,3,128,128]{4,3,2,1,0:T(8,128)(2,1)} %weight_in.1, f32[1,128]{1,0:T(1,128)} %bitcast.10, f32[1,128]{1,0:T(1,128)} %bitcast.11, bf16[4,32,128]{2,1,0:T(8,128)(2,1)} %bitcast.7), custom_call_target="tpu_custom_call" | custom-call | tf_op jit(solution)/shard_map/pallas_call | solution.py:599
  25.6 0.6 %copy.9 = bf16[1,16,16,128]{3,2,1,0:T(8,128)(2,1)} copy(bf16[1,16,16,128]{3,2,1,0:T(8,128)(2,1)S(1)} %shard_map.73) | data formatting | bytes 131072

commit v3 on v2

--- a/solution.py
+++ b/solution.py
@@ -39,6 +39,7 @@
     has_main = jnp.logical_or(c == 1, t < n_tm - 1)
     mirror = n_space == 2
     flip = s == 0 if mirror else False
+    window = 4
     rounds = max(n_tm // 2 + n_space - 1, n_tm - 1) - 1
 
     def row_of(p):
@@ -123,7 +124,7 @@
         begin = 1 + (jnp.where(flip, rows - p - count, p) if mirror else p)
         return remote(
             x.at[c + frame, pl.ds(begin, count), c], x.at[slot, pl.ds(begin, count), c],
-            z_send.at[int(up)], z_recv.at[p], {"tm": tt, "space": s, "chan": core},
+            z_send.at[int(up), p % window], z_recv.at[p], {"tm": tt, "space": s, "chan": core},
         )
 
     def meta_copy(up):
@@ -157,26 +158,41 @@
     zs = ((True, up_ok), (False, down_ok))
     sides = ((True, low_ok), (False, high_ok))
 
-    for p in range(2):
+    def start_z(p):
         for up, ok in zs:
             @pl.when(ok)
-            def _(up=up, p=p):
+            def _(up=up):
                 z_copy(up, p, 1).start()
-    peer.start()
-    for low, ok in sides:
-        @pl.when(ok)
-        def _(low=low):
-            edge(low, 0).start()
-            edge(low, 1).start()
-    for up, ok in zs:
-        @pl.when(ok)
-        def _(up=up):
-            meta_copy(up).start()
-    for p in range(2, rows):
+
+    def start_edges():
+        for low, ok in sides:
+            @pl.when(ok)
+            def _(low=low):
+                edge(low, 0).start()
+                edge(low, 1).start()
+
+    def start_meta():
         for up, ok in zs:
             @pl.when(ok)
-            def _(up=up, p=p):
-                z_copy(up, p, 1).start()
+            def _(up=up):
+                meta_copy(up).start()
+
+    start_meta()
+    peer.start()
+    start_z(0)
+    start_z(1)
+    start_z(2)
+    start_z(3)
+    start_edges()
+
+    def advance(p):
+        if p + window < rows:
+            for up, ok in zs:
+                @pl.when(ok)
+                def _(up=up):
+                    z_copy(up, p, 1).wait_send()
+                    z_copy(up, p + window, 1).start()
+
     if rounds > 0:
         greet(round_sem.at[0])
 
@@ -184,7 +200,8 @@
     for k in range(3):
         for i in range(3):
             for j in range(3):
-                wt[k, pl.ds(j * 128, 128), pl.ds(i * 128, 128)] = weight[k, i, j].T
+                wt[pl.ds(j * 128, 128), pl.ds((3 * k + i) * 128, 128)] = weight[k, i, j].T
+    advance(0)
     for fetch in fetches[4:]:
         fetch.wait()
 
@@ -204,6 +221,7 @@
     )
 
     peer.wait_recv()
+    advance(1)
     if rounds > 0:
         pl.semaphore_wait(round_sem.at[0], near_count)
 
@@ -218,18 +236,22 @@
     lane = lax.broadcasted_iota(jnp.int32, (CHANNELS, columns), 1)
 
     def conv_row(h, kept, taps):
-        acc = None
-        for k in range(3):
-            term = jnp.dot(wt[k], taps[k](h), preferred_element_type=F32)
-            acc = term if acc is None else acc + term
+        acc = jnp.dot(
+            wt[...], jnp.concatenate([tap(h) for tap in taps], axis=0),
+            preferred_element_type=F32,
+        )
         left = jnp.where(lane == 0, 0.0, pltpu.roll(acc[0:128], 1, 1))
         right = jnp.where(lane == columns - 1, 0.0, pltpu.roll(acc[256:384], columns - 1, 1))
         value = (left + acc[128:256] + right).astype(BF16)
         conv[kept, h] = value
         value = value.astype(F32)
         a, b = value[:, :lanes], value[:, lanes:]
-        sums[0] += a + b
-        sums[1] += a * a + b * b
+        return a + b, a * a + b * b
+
+    def conv_pair(h, later, kept, taps):
+        one, two = conv_row(h, kept, taps), conv_row(later, kept, taps)
+        sums[0] += one[0] + two[0]
+        sums[1] += one[1] + two[1]
 
     def slab(slot):
         return lambda h: x[slot, pl.ds(h, 3)].reshape(3 * CHANNELS, columns)
@@ -291,16 +313,21 @@
     def _():
         sums[...] = jnp.zeros_like(sums)
 
-        @pl.loop(0, half_rows)
+        @pl.loop(0, half_rows // 2)
         def _(n):
             if mirror:
-                @pl.when(jnp.logical_and(c == 1, n == half_rows - 1))
+                @pl.when(n == half_rows // 2 - 1)
                 def _():
-                    wait_edges()
-            p = half_rows - 1 - n + jnp.where(c == 0, half_rows, 0) if mirror else (
-                n + c * half_rows
+                    for p in range(2, rows):
+                        advance(p)
+
+                    @pl.when(c == 1)
+                    def _():
+                        wait_edges()
+            p = half_rows - 1 - 2 * n + jnp.where(c == 0, half_rows, 0) if mirror else (
+                2 * n + 1 + c * half_rows
             )
-            conv_row(row_of(p), 1, [slab(c)] * 3)
+            conv_pair(row_of(p), row_of(p - 1), 1, [slab(c)] * 3)
 
         sums_to(3)
 
@@ -311,7 +338,12 @@
         return jnp.where(newer, slab(1)(h), slab(2)(h))
 
     taps = [tap_old, tap_mid, slab(2)]
-    border_step = rows - 4
+    steps = rows // 2
+
+    @pl.when(jnp.logical_not(first) if mirror else True)
+    def _():
+        for p in range(2, rows):
+            advance(p)
 
     if mirror:
         wait_z(0)
@@ -325,31 +357,35 @@
 
     sums[...] = jnp.zeros_like(sums)
 
-    @pl.loop(0, rows)
+    @pl.loop(0, steps)
     def _(n):
         if mirror:
-            @pl.when(n < border_step)
+            @pl.when(n < steps - 2)
             def _():
-                wait_z(n + 2)
-
-            @pl.when(n == border_step)
+                wait_z(2 * n + 2)
+                wait_z(2 * n + 3)
+
+            @pl.when(n == steps - 2)
             def _():
+                wait_z(rows - 2)
+
                 @pl.when(jnp.logical_not(jnp.logical_and(first, c == 1)))
                 def _():
                     wait_edges()
                 wait_forwards()
 
-            @pl.when(jnp.logical_and(n > border_step, n < rows - 1))
+            @pl.when(n == steps - 1)
             def _():
-                wait_z(n + 1)
-
-            p = jnp.where(n < border_step, n + 1, jnp.where(n == border_step, 0, n))
+                wait_z(rows - 1)
+
+            p = jnp.where(n == steps - 1, rows - 2, 2 * n + 1)
+            later = jnp.where(n < steps - 2, 2 * n + 2, jnp.where(n == steps - 2, 0, rows - 1))
         else:
-            p = n
+            p, later = 2 * n, 2 * n + 1
 
         @pl.when(has_main)
         def _():
-            conv_row(row_of(p), 0, taps)
+            conv_pair(row_of(p), row_of(later), 0, taps)
 
     @pl.when(has_main)
     def _():
@@ -554,7 +590,8 @@
     for up, ok in zs:
         @pl.when(ok)
         def _(up=up):
-            z_copy(up, 0, rows).wait_send()
+            for p in range(rows - window, rows):
+                z_copy(up, p, 1).wait_send()
             meta_copy(up).wait_send()
     for low, ok in sides:
         @pl.when(ok)
@@ -615,7 +652,7 @@
                 pltpu.VMEM((2, 8, 128), jnp.int32),
                 pltpu.SMEM((2, 8, 128), jnp.int32),
                 pltpu.VMEM((3, rows + 2, 2, half, columns), BF16),
-                pltpu.VMEM((3, 384, 384), BF16),
+                pltpu.VMEM((384, 1152), BF16),
                 pltpu.VMEM((2, rows, CHANNELS, columns), BF16),
                 pltpu.VMEM((8, 128), F32),
                 pltpu.VMEM((total, 8, 128), F32),
@@ -624,7 +661,7 @@
                 pltpu.VMEM((n_tm * frames_here * lat_rows, moments // 2, columns // 2), BF16),
                 pltpu.VMEM((2, CHANNELS, columns // 2), F32),
                 pltpu.SemaphoreType.REGULAR((2,)),
-                dma((2,)),
+                dma((2, 4)),
                 dma((rows,)),
                 dma((2,)),
                 dma((2,)),

time: 26.4 us -> 24.3 us (0.920)
  Pallas kernels: 25.6 us -> 23.5 us
    pallas_call x1, Pallas kernels: 25.6 us -> 23.5 us  [shards(): pl.pallas_call(functools.partial(kernel, (n_tm, n_space, capacity)), out_...]
where the time goes in v3:
time: 24.3 us; the launch traced here: 24.2 us
  Pallas kernels  23.5 us (97%)
  local copies, waits for them, and re-layouts  0.63 us (3%)
    pallas_call x1, Pallas kernels, shards(): pl.pallas_call(functools.partial(kernel, (n_tm, n_space, capacity)), out_...  23.5 us
    unnamed x1, local copies, waits for them, and re-layouts  0.63 us

profile of v3, /device:TPU:0, one launch (start us, length us, event | category | flops | bytes accessed | tf_op | source)
XLA Modules:
  0.0 24.2 jit_solution(11295758656204372510)
XLA Ops:
  0.0 23.5 %shard_map.73 = bf16[1,16,16,128]{3,2,1,0:T(8,128)(2,1)S(1)} custom-call(s32[1,2]{1,0:T(1,128)} %bitcast.8, s32[1,8]{1,0:T(1,128)} %bitcast.9, bf16[64,2,8,256]{3,2,1,0:T(8,128)(2,1)} %act_in.1, bf16[3,3,3,128,128]{4,3,2,1,0:T(8,128)(2,1)} %weight_in.1, f32[1,128]{1,0:T(1,128)} %bitcast.10, f32[1,128]{1,0:T(1,128)} %bitcast.11, bf16[4,32,128]{2,1,0:T(8,128)(2,1)} %bitcast.7), custom_call_target="tpu_custom_call" | custom-call | tf_op jit(solution)/shard_map/pallas_call | solution.py:636
  23.6 0.6 %copy.9 = bf16[1,16,16,128]{3,2,1,0:T(8,128)(2,1)} copy(bf16[1,16,16,128]{3,2,1,0:T(8,128)(2,1)S(1)} %shard_map.73) | data formatting | bytes 131072

commit v4 on v2

--- a/solution.py
+++ b/solution.py
@@ -17,10 +17,10 @@
 
 def kernel(
     sizes, clip_hbm, owner_hbm, act_in, weight_in, gain_in, bias_in, out_weight_in, out,
-    clip_in, owner_in, act_raw, weight, gain, bias, out_weight, meta_in, near_meta, near_ids,
+    clip_in, owner_in, act_raw, weight, gain, bias, out_weight, meta_in, near_meta, near_ids, meta,
     x, wt, conv, stat, stats, ids, latent, arrived, sums,
     round_sem, z_send, z_recv, edge_send, edge_recv, fwd_send, fwd_recv, peer_send, peer_recv,
-    meta_send, meta_recv, stat_send, stat_recv, lat_send, lat_recv, local_sem,
+    meta_send, meta_recv, owner_send, owner_recv, stat_send, stat_recv, lat_send, lat_recv, local_sem,
 ):
     n_tm, n_space, capacity = sizes
     half, frames_here, rows, columns = act_raw.shape
@@ -41,6 +41,13 @@
     flip = s == 0 if mirror else False
     rounds = max(n_tm // 2 + n_space - 1, n_tm - 1) - 1
 
+    def repeat(count, body):
+        if count <= 4:
+            for n in range(count):
+                body(n)
+        else:
+            pl.loop(0, count)(body)
+
     def row_of(p):
         return jnp.where(flip, rows - 1 - p, p) if mirror else p
 
@@ -51,7 +58,7 @@
             (gain_in, gain), (bias_in, bias), (out_weight_in, out_weight),
         ))
     ]
-    for fetch in fetches:
+    for fetch in fetches[:3]:
         fetch.start()
     stats[...] = jnp.full(stats.shape, -1.0, F32)
 
@@ -96,7 +103,10 @@
     numbers = jnp.zeros((8, 128), jnp.int32)
     for n in range(frames_here):
         numbers = jnp.where(place == n, clip_in[0, n], numbers)
+    for n in range(own_rows):
+        numbers = jnp.where(place == frames_here + n, owner_in[0, n], numbers)
     meta_in[...] = numbers
+    meta[t] = numbers
 
     @pl.when(first)
     def _():
@@ -106,9 +116,19 @@
     def _():
         near_meta[1] = numbers
 
+    split_row = lax.broadcasted_iota(jnp.int32, (columns, columns), 0)
+    split_col = lax.broadcasted_iota(jnp.int32, (columns, columns), 1)
+    picked = jnp.where(split_col < lanes, 2 * split_col, 2 * (split_col - lanes) + 1)
+    split = jnp.where(split_row == picked, 1.0, 0.0).astype(BF16)
+
     fetches[0].wait()
+    for fetch in fetches[3:]:
+        fetch.start()
     for f in range(frames_here):
-        x[c + f, pl.ds(1, rows), c] = jnp.transpose(act_raw[:, f], (1, 0, 2))
+        turned = jnp.transpose(act_raw[:, f], (1, 0, 2)).reshape(rows * half, columns)
+        x[c + f, pl.ds(1, rows), c] = jnp.dot(
+            turned, split, preferred_element_type=F32
+        ).astype(BF16).reshape(rows, half, columns)
 
     pl.semaphore_wait(barrier, near_count)
 
@@ -157,26 +177,27 @@
     zs = ((True, up_ok), (False, down_ok))
     sides = ((True, low_ok), (False, high_ok))
 
-    for p in range(2):
+    def start_z(p):
         for up, ok in zs:
             @pl.when(ok)
-            def _(up=up, p=p):
+            def _(up=up):
                 z_copy(up, p, 1).start()
+
+    for up, ok in zs:
+        @pl.when(ok)
+        def _(up=up):
+            meta_copy(up).start()
     peer.start()
+    start_z(0)
+    start_z(1)
     for low, ok in sides:
         @pl.when(ok)
         def _(low=low):
             edge(low, 0).start()
             edge(low, 1).start()
-    for up, ok in zs:
-        @pl.when(ok)
-        def _(up=up):
-            meta_copy(up).start()
     for p in range(2, rows):
-        for up, ok in zs:
-            @pl.when(ok)
-            def _(up=up, p=p):
-                z_copy(up, p, 1).start()
+        start_z(p)
+
     if rounds > 0:
         greet(round_sem.at[0])
 
@@ -184,7 +205,7 @@
     for k in range(3):
         for i in range(3):
             for j in range(3):
-                wt[k, pl.ds(j * 128, 128), pl.ds(i * 128, 128)] = weight[k, i, j].T
+                wt[pl.ds(j * 128, 128), pl.ds((3 * k + i) * 128, 128)] = weight[k, i, j].T
     for fetch in fetches[4:]:
         fetch.wait()
 
@@ -215,21 +236,31 @@
             def _():
                 pl.semaphore_wait(round_sem.at[lax.rem(r, 2)], near_count)
 
-    lane = lax.broadcasted_iota(jnp.int32, (CHANNELS, columns), 1)
+    lane = lax.broadcasted_iota(jnp.int32, (CHANNELS, lanes), 1)
 
     def conv_row(h, kept, taps):
-        acc = None
-        for k in range(3):
-            term = jnp.dot(wt[k], taps[k](h), preferred_element_type=F32)
-            acc = term if acc is None else acc + term
-        left = jnp.where(lane == 0, 0.0, pltpu.roll(acc[0:128], 1, 1))
-        right = jnp.where(lane == columns - 1, 0.0, pltpu.roll(acc[256:384], columns - 1, 1))
-        value = (left + acc[128:256] + right).astype(BF16)
-        conv[kept, h] = value
-        value = value.astype(F32)
-        a, b = value[:, :lanes], value[:, lanes:]
-        sums[0] += a + b
-        sums[1] += a * a + b * b
+        acc = jnp.dot(
+            wt[...], jnp.concatenate([tap(h) for tap in taps], axis=0),
+            preferred_element_type=F32,
+        )
+        even, odd = acc[:, :lanes], acc[:, lanes:]
+        before = jnp.where(lane == 0, 0.0, pltpu.roll(odd[0:128], 1, 1))
+        after = jnp.where(lane == lanes - 1, 0.0, pltpu.roll(even[256:384], lanes - 1, 1))
+        even, odd = (
+            (before + even[128:256] + odd[256:384]).astype(BF16),
+            (even[0:128] + odd[128:256] + after).astype(BF16),
+        )
+        conv[kept, h] = jnp.concatenate([even, odd], axis=1)
+        a, b = even.astype(F32), odd.astype(F32)
+        return a + b, a * a + b * b
+
+    def conv_rows(places, kept, taps):
+        found = [conv_row(h, kept, taps) for h in places]
+        for q in range(2):
+            total_q = found[0][q]
+            for one in found[1:]:
+                total_q = total_q + one[q]
+            sums[q] += total_q
 
     def slab(slot):
         return lambda h: x[slot, pl.ds(h, 3)].reshape(3 * CHANNELS, columns)
@@ -276,10 +307,6 @@
     facts = jnp.where(
         jnp.logical_and(row8 == 5, first), clip_in[0, 0].astype(F32), facts
     )
-    for n in range(own_rows):
-        facts = jnp.where(
-            jnp.logical_and(row8 == 6, lane8 == n), owner_in[0, n].astype(F32), facts
-        )
     stat[...] = facts
 
     half_index = jnp.where(flip, c, 1 - c) if mirror else c
@@ -291,17 +318,14 @@
     def _():
         sums[...] = jnp.zeros_like(sums)
 
-        @pl.loop(0, half_rows)
-        def _(n):
-            if mirror:
-                @pl.when(jnp.logical_and(c == 1, n == half_rows - 1))
-                def _():
-                    wait_edges()
-            p = half_rows - 1 - n + jnp.where(c == 0, half_rows, 0) if mirror else (
-                n + c * half_rows
-            )
-            conv_row(row_of(p), 1, [slab(c)] * 3)
-
+        if mirror:
+            @pl.when(c == 1)
+            def _():
+                wait_edges()
+        begin = jnp.where(c == 0, half_rows, 0) if mirror else c * half_rows
+        conv_rows(
+            [row_of(begin + p) for p in range(half_rows - 1, -1, -1)], 1, [slab(c)] * 3
+        )
         sums_to(3)
 
     def tap_old(h):
@@ -311,7 +335,23 @@
         return jnp.where(newer, slab(1)(h), slab(2)(h))
 
     taps = [tap_old, tap_mid, slab(2)]
-    border_step = rows - 4
+    steps = rows // 2
+
+    def send_owners():
+        def to(n):
+            remote(
+                meta_in, meta.at[t], owner_send.at[0], owner_recv.at[0],
+                {"tm": lax.rem(t + 1 + n, n_tm), "space": s, "chan": c},
+            ).start()
+
+        repeat(n_tm - 1, to)
+
+    def owner_wait(received):
+        span = meta.at[pl.ds(0, n_tm - 1)]
+        copy = remote(
+            span, span, owner_send.at[0], owner_recv.at[0], {"tm": t, "space": s, "chan": c}
+        )
+        copy.wait_recv() if received else copy.wait_send()
 
     if mirror:
         wait_z(0)
@@ -325,98 +365,94 @@
 
     sums[...] = jnp.zeros_like(sums)
 
-    @pl.loop(0, rows)
+    @pl.loop(0, steps - 2)
     def _(n):
         if mirror:
-            @pl.when(n < border_step)
-            def _():
-                wait_z(n + 2)
-
-            @pl.when(n == border_step)
-            def _():
-                @pl.when(jnp.logical_not(jnp.logical_and(first, c == 1)))
-                def _():
-                    wait_edges()
-                wait_forwards()
-
-            @pl.when(jnp.logical_and(n > border_step, n < rows - 1))
-            def _():
-                wait_z(n + 1)
-
-            p = jnp.where(n < border_step, n + 1, jnp.where(n == border_step, 0, n))
-        else:
-            p = n
+            wait_z(2 * n + 2)
+            wait_z(2 * n + 3)
 
         @pl.when(has_main)
         def _():
-            conv_row(row_of(p), 0, taps)
+            conv_rows([row_of(2 * n + 1), row_of(2 * n + 2)], 0, taps)
+
+    if mirror:
+        @pl.when(jnp.logical_not(jnp.logical_and(first, c == 1)))
+        def _():
+            wait_edges()
+        wait_z(rows - 2)
+        wait_forwards()
+        wait_z(rows - 1)
 
     @pl.when(has_main)
     def _():
+        conv_rows([row_of(p) for p in (rows - 3, 0, rows - 2, rows - 1)], 0, taps)
+
+    @pl.when(has_main)
+    def _():
         sums_to(0)
 
+    stats[me] = stat[...]
     if rounds > 1:
         pl.semaphore_wait(round_sem.at[(rounds - 1) % 2], near_count)
 
-    stats[me] = stat[...]
-
-    def needs(tt, ss, core):
-        apart = jnp.abs(2 * (tt - t) + c - core) <= n_tm - 1
-        return jnp.logical_or(apart, jnp.logical_and(ss == s, core == c))
-
     def stat_copy(tt, ss, core):
-        target = (tt * n_space + ss) * 2 + core
         return remote(
-            stat, stats.at[me], stat_send.at[target], stat_recv.at[me],
+            stat, stats.at[me], stat_send.at[0], stat_recv.at[0],
             {"tm": tt, "space": ss, "chan": core},
         )
 
-    def stat_from(tt, ss, core):
-        source = (tt * n_space + ss) * 2 + core
-        return remote(
-            stat, stats.at[source], stat_send.at[source], stat_recv.at[source],
-            {"tm": tt, "space": ss, "chan": core},
-        )
-
-    def each_stat(act):
-        @pl.loop(0, n_tm)
-        def _(step):
-            far = n_tm - 1 - step
-            for up in (True, False):
-                tt = t + far if up else t - far
-                ok = jnp.logical_and(tt < n_tm, tt >= 0)
-                if not up:
-                    ok = jnp.logical_and(ok, far > 0)
-                for ss in range(n_space):
-                    for core in range(2):
-                        use = jnp.logical_and(ok, needs(tt, ss, core))
-                        other = (tt * n_space + ss) * 2 + core != me
-
-                        @pl.when(jnp.logical_and(use, other))
-                        def _(tt=tt, ss=ss, core=core):
-                            act(tt, ss, core)
-
-    each_stat(lambda tt, ss, core: stat_copy(tt, ss, core).start())
-
-    spread_row = lax.broadcasted_iota(jnp.int32, (columns, lanes), 0)
-    spread_col = lax.broadcasted_iota(jnp.int32, (columns, lanes), 1)
-    spread = jnp.where(spread_row == 2 * spread_col, 1.0, 0.0).astype(BF16)
-    weights = jnp.concatenate(
-        [
-            jnp.concatenate([out_weight[2 * i + j] for i in range(2)], axis=1)
-            for j in range(2)
-        ],
-        axis=0,
-    )
-
-    each_stat(lambda tt, ss, core: stat_from(tt, ss, core).wait_recv())
-
-    owners = [
-        pltpu.make_async_copy(stats.at[(b * n_space + s) * 2 + c], ids.at[b], local_sem.at[8])
-        for b in range(n_tm)
-    ]
-    for copy in owners:
-        copy.start()
+    reach = n_tm // 2
+
+    def spaces(act):
+        repeat(n_space, lambda n: act(lax.rem(s + n_space - 1 - n, n_space), n))
+
+    far_t = jnp.where(c == 0, t + reach, t - reach)
+
+    @pl.when(jnp.logical_and(far_t >= 0, far_t < n_tm))
+    def _():
+        spaces(lambda ss, n: stat_copy(far_t, ss, 1 - c).start())
+
+    def slab_both(away):
+        for tt in (t + away, t - away):
+            @pl.when(jnp.logical_and(tt >= 0, tt < n_tm))
+            def _(tt=tt):
+                for core in range(2):
+                    spaces(lambda ss, n: stat_copy(tt, ss, core).start())
+
+    repeat(reach - 1, lambda n: slab_both(reach - 1 - n))
+    repeat(n_space - 1, lambda n: [
+        stat_copy(t, lax.rem(s + 1 + n, n_space), core).start() for core in range(2)
+    ] and None)
+    stat_copy(t, s, 1 - c).start()
+    send_owners()
+
+    stat_counts = {
+        (tt, core): 2 * n_space - 1 + sum(
+            n_space * len([o for o in (0, 1) if abs(2 * (other - tt) + core - o) < n_tm])
+            for other in range(n_tm) if other != tt
+        )
+        for tt in range(n_tm) for core in range(2)
+    }
+
+    def stat_wait(received):
+        for count in sorted(set(stat_counts.values())):
+            same = False
+            for (tt, core), number in stat_counts.items():
+                if number == count:
+                    same = jnp.logical_or(same, jnp.logical_and(t == tt, c == core))
+
+            @pl.when(same)
+            def _(count=count):
+                span = stats.at[pl.ds(0, count)]
+                copy = remote(
+                    span, span, stat_send.at[0], stat_recv.at[0],
+                    {"tm": t, "space": s, "chan": c},
+                )
+                copy.wait_recv() if received else copy.wait_send()
+
+    weights = jnp.concatenate([out_weight[q] for q in range(4)], axis=1)
+
+    stat_wait(True)
 
     sizes_row = jnp.where(
         row8 == 2, float(rows * columns), float(half_rows * columns)
@@ -453,66 +489,60 @@
         shift = bias[...] * 0.5 - mean * scale
         return jnp.broadcast_to(scale, (128, 128)).T, jnp.broadcast_to(shift, (128, 128)).T
 
-    def finish(kept, begin, scale_c, shift_c):
-        packed = []
-        for r in range(piece_rows):
-            pair = []
+    def finish(kept, begin, count, scale_c, shift_c):
+        wide = []
+        for r in range(count):
+            pieces = []
             for i in range(2):
                 value = conv[kept, 2 * (begin + r) + i].astype(F32)
-                pieces = []
-                for u in range(2):
-                    v = value[:, u * lanes:(u + 1) * lanes] * scale_c + shift_c
+                for j in range(2):
+                    v = value[:, j * lanes:(j + 1) * lanes] * scale_c + shift_c
                     pieces.append((v + v * jnp.tanh(v)).astype(BF16))
-                pair.append(jnp.concatenate(pieces, axis=1))
-            both = jnp.dot(
-                weights, jnp.concatenate(pair, axis=0), preferred_element_type=F32
-            )
-            packed.append((both[0:32] + pltpu.roll(both[32:64], columns - 1, 1)).astype(BF16))
+            wide.append(jnp.concatenate(pieces, axis=0))
         result = jnp.dot(
-            jnp.concatenate(packed, axis=0), spread, preferred_element_type=F32
+            weights, jnp.concatenate(wide, axis=1), preferred_element_type=F32
         ).astype(BF16)
-        for r in range(piece_rows):
+        for r in range(count):
             for core in range(2):
-                latent[kept, core, begin + r] = result[r * 32 + core * 16:r * 32 + core * 16 + 16]
-
-    def send_latent(kept, begin, frame):
-        span = pl.ds(frame * lat_rows + begin, piece_rows)
-        arrived[span] = latent[kept, c, pl.ds(begin, piece_rows)]
-
-        @pl.loop(0, n_tm)
-        def _(step):
-            far = n_tm - 1 - step
-            for up in (True, False):
-                tt = t + far if up else t - far
-                ok = jnp.logical_and(tt < n_tm, tt >= 0)
-                if not up:
-                    ok = jnp.logical_and(ok, far > 0)
-                for core in range(2):
-                    other = jnp.logical_or(tt != t, core != c)
-
-                    @pl.when(jnp.logical_and(ok, other))
-                    def _(tt=tt, core=core):
-                        remote(
-                            latent.at[kept, core, pl.ds(begin, piece_rows)], arrived.at[span],
-                            lat_send.at[kept], lat_recv.at[0],
-                            {"tm": tt, "space": s, "chan": core},
-                        ).start()
+                latent[kept, core, begin + r] = result[
+                    core * 16:core * 16 + 16, r * lanes:(r + 1) * lanes
+                ]
+
+    def send_latent(kept, begin, count, frame):
+        span = pl.ds(frame * lat_rows + begin, count)
+        arrived[span] = latent[kept, c, pl.ds(begin, count)]
+
+        def to(tt, core):
+            remote(
+                latent.at[kept, core, pl.ds(begin, count)], arrived.at[span],
+                lat_send.at[kept], lat_recv.at[0], {"tm": tt, "space": s, "chan": core},
+            ).start()
+
+        def others(n):
+            step = jnp.where(t < n_tm // 2, n_tm - 1 - n, 1 + n)
+            for core in range(2):
+                to(lax.rem(t + step, n_tm), core)
+
+        repeat(n_tm - 1, others)
+        to(t, 1 - c)
 
     my_frame = 2 * t + 2 - c
 
     @pl.when(first)
     def _():
-        finish(1, half_index * piece_rows, *moments_of(clip_in[0, 0]))
-        send_latent(1, half_index * piece_rows, 0)
+        finish(1, half_index * piece_rows, piece_rows, *moments_of(clip_in[0, 0]))
+        send_latent(1, half_index * piece_rows, piece_rows, 0)
 
     @pl.when(has_main)
     def _():
         found = moments_of(my_clip)
-        for piece in range(2):
-            finish(0, piece * piece_rows, *found)
-            send_latent(0, piece * piece_rows, my_frame)
-
-    pltpu.make_async_copy(stats.at[pl.ds(0, n_tm)], ids, local_sem.at[8]).wait()
+        finish(0, 0, lat_rows, *found)
+        send_latent(0, 0, lat_rows, my_frame)
+
+    owner_wait(True)
+    owners = pltpu.make_async_copy(meta, ids, local_sem.at[8])
+    owners.start()
+    owners.wait()
 
     def arrived_wait(count):
         span = arrived.at[pl.ds(0, count)]
@@ -534,14 +564,12 @@
     def _():
         arrived_wait(every)
 
-    here = t.astype(F32)
-
     @pl.loop(0, n_tm)
     def _(b):
         taken = jnp.int32(0)
         slots = []
         for n in range(own_rows):
-            hit = ids[b, 6, n] == here
+            hit = ids[b, 0, frames_here + n] == t
             slots.append(jnp.where(hit, taken, -1))
             taken = taken + jnp.where(hit, 1, 0)
         for j in range(capacity):
@@ -569,7 +597,8 @@
             def _():
                 forward(low).wait_send()
 
-    each_stat(lambda tt, ss, core: stat_copy(tt, ss, core).wait_send())
+    stat_wait(False)
+    owner_wait(False)
 
     def latents_left(kept, count):
         span = arrived.at[pl.ds(0, count)]
@@ -614,12 +643,13 @@
                 pltpu.VMEM((8, 128), jnp.int32),
                 pltpu.VMEM((2, 8, 128), jnp.int32),
                 pltpu.SMEM((2, 8, 128), jnp.int32),
+                pltpu.VMEM((n_tm, 8, 128), jnp.int32),
                 pltpu.VMEM((3, rows + 2, 2, half, columns), BF16),
-                pltpu.VMEM((3, 384, 384), BF16),
+                pltpu.VMEM((384, 1152), BF16),
                 pltpu.VMEM((2, rows, CHANNELS, columns), BF16),
                 pltpu.VMEM((8, 128), F32),
                 pltpu.VMEM((total, 8, 128), F32),
-                pltpu.SMEM((n_tm, 8, 128), F32),
+                pltpu.SMEM((n_tm, 8, 128), jnp.int32),
                 pltpu.VMEM((2, 2, lat_rows, moments // 2, columns // 2), BF16),
                 pltpu.VMEM((n_tm * frames_here * lat_rows, moments // 2, columns // 2), BF16),
                 pltpu.VMEM((2, CHANNELS, columns // 2), F32),
@@ -634,8 +664,10 @@
                 dma((1,)),
                 dma((2,)),
                 dma((2,)),
-                dma((total,)),
-                dma((total,)),
+                dma((1,)),
+                dma((1,)),
+                dma((1,)),
+                dma((1,)),
                 dma((2,)),
                 dma((1,)),
                 dma((9,)),

time: 26.4 us -> 22.8 us (0.86)
  Pallas kernels: 25.6 us -> 22 us
    pallas_call x1, Pallas kernels: 25.6 us -> 22 us  [shards(): pl.pallas_call(functools.partial(kernel, (n_tm, n_space, capacity)), out_...]
where the time goes in v4:
time: 22.8 us; the launch traced here: 22.7 us
  Pallas kernels  22 us (96%)
  local copies, waits for them, and re-layouts  0.63 us (3%)
    pallas_call x1, Pallas kernels, shards(): pl.pallas_call(functools.partial(kernel, (n_tm, n_space, capacity)), out_...  22 us
    unnamed x1, local copies, waits for them, and re-layouts  0.63 us

profile of v4, /device:TPU:0, one launch (start us, length us, event | category | flops | bytes accessed | tf_op | source)
XLA Modules:
  0.0 22.7 jit_solution(15670114538349803604)
XLA Ops:
  0.0 22.0 %shard_map.73 = bf16[1,16,16,128]{3,2,1,0:T(8,128)(2,1)S(1)} custom-call(s32[1,2]{1,0:T(1,128)} %bitcast.8, s32[1,8]{1,0:T(1,128)} %bitcast.9, bf16[64,2,8,256]{3,2,1,0:T(8,128)(2,1)} %act_in.1, bf16[3,3,3,128,128]{4,3,2,1,0:T(8,128)(2,1)} %weight_in.1, f32[1,128]{1,0:T(1,128)} %bitcast.10, f32[1,128]{1,0:T(1,128)} %bitcast.11, bf16[4,32,128]{2,1,0:T(8,128)(2,1)} %bitcast.7), custom_call_target="tpu_custom_call" | custom-call | tf_op jit(solution)/shard_map/pallas_call | solution.py:628
  22.0 0.6 %copy.9 = bf16[1,16,16,128]{3,2,1,0:T(8,128)(2,1)} copy(bf16[1,16,16,128]{3,2,1,0:T(8,128)(2,1)S(1)} %shard_map.73) | data formatting | bytes 131072

commit v5 on v4

--- a/solution.py
+++ b/solution.py
@@ -18,7 +18,7 @@
 def kernel(
     sizes, clip_hbm, owner_hbm, act_in, weight_in, gain_in, bias_in, out_weight_in, out,
     clip_in, owner_in, act_raw, weight, gain, bias, out_weight, meta_in, near_meta, near_ids, meta,
-    x, wt, conv, stat, stats, ids, latent, arrived, sums,
+    x, wt, wz, acc, conv, stat, stats, ids, latent, arrived, sums,
     round_sem, z_send, z_recv, edge_send, edge_recv, fwd_send, fwd_recv, peer_send, peer_recv,
     meta_send, meta_recv, owner_send, owner_recv, stat_send, stat_recv, lat_send, lat_recv, local_sem,
 ):
@@ -61,6 +61,7 @@
     for fetch in fetches[:3]:
         fetch.start()
     stats[...] = jnp.full(stats.shape, -1.0, F32)
+    stat[...] = jnp.full(stat.shape, -1.0, F32)
 
     up_ok, down_ok = t < n_tm - 1, t > 0
     low_ok, high_ok = s > 0, s < n_space - 1
@@ -97,6 +98,10 @@
     def _():
         x[:, rows + 1] = zero_row
 
+    @pl.when(jnp.logical_and(first, c == 1))
+    def _():
+        x[0] = jnp.zeros((rows + 2, 2, half, columns), BF16)
+
     fetches[1].wait()
     fetches[2].wait()
     place = lax.broadcasted_iota(jnp.int32, (8, 128), 1)
@@ -108,13 +113,13 @@
     meta_in[...] = numbers
     meta[t] = numbers
 
-    @pl.when(first)
-    def _():
-        near_meta[0] = numbers
-
-    @pl.when(t == n_tm - 1)
-    def _():
-        near_meta[1] = numbers
+    gets_z = jnp.logical_or(
+        jnp.logical_and(c == 0, up_ok), jnp.logical_and(c == 1, down_ok)
+    )
+
+    @pl.when(jnp.logical_not(gets_z))
+    def _():
+        near_meta[...] = numbers
 
     split_row = lax.broadcasted_iota(jnp.int32, (columns, columns), 0)
     split_col = lax.broadcasted_iota(jnp.int32, (columns, columns), 1)
@@ -146,12 +151,13 @@
             z_send.at[int(up)], z_recv.at[p], {"tm": tt, "space": s, "chan": core},
         )
 
-    def meta_copy(up):
-        return remote(
-            meta_in, near_meta.at[0 if up else 1], meta_send.at[int(up)],
-            meta_recv.at[0 if up else 1],
-            {"tm": t_up if up else t_down, "space": s, "chan": c},
-        )
+    meta_copy = remote(
+        meta_in, near_meta, meta_send.at[0], meta_recv.at[0],
+        {"tm": jnp.where(c == 0, t_down, t_up), "space": s, "chan": c},
+    )
+    meta_sent = jnp.logical_or(
+        jnp.logical_and(c == 0, down_ok), jnp.logical_and(c == 1, up_ok)
+    )
 
     def edge(low, core):
         return remote(
@@ -183,10 +189,10 @@
             def _(up=up):
                 z_copy(up, p, 1).start()
 
-    for up, ok in zs:
-        @pl.when(ok)
-        def _(up=up):
-            meta_copy(up).start()
+    @pl.when(meta_sent)
+    def _():
+        meta_copy.start()
+
     peer.start()
     start_z(0)
     start_z(1)
@@ -209,21 +215,6 @@
     for fetch in fetches[4:]:
         fetch.wait()
 
-    for up, ok in zs:
-        @pl.when(ok)
-        def _(up=up):
-            meta_copy(not up).wait_recv()
-    to_scalars = pltpu.make_async_copy(near_meta, near_ids, local_sem.at[7])
-    to_scalars.start()
-    to_scalars.wait()
-
-    my_clip = jnp.where(c == 1, clip_in[0, 1], near_ids[1, 0, 0])
-    newer = jnp.where(c == 1, clip_in[0, 0], clip_in[0, 1]) == my_clip
-    older = jnp.logical_and(
-        jnp.logical_or(c == 0, t > 0),
-        jnp.where(c == 1, near_ids[0, 0, 1], clip_in[0, 0]) == my_clip,
-    )
-
     peer.wait_recv()
     if rounds > 0:
         pl.semaphore_wait(round_sem.at[0], near_count)
@@ -238,12 +229,27 @@
 
     lane = lax.broadcasted_iota(jnp.int32, (CHANNELS, lanes), 1)
 
-    def conv_row(h, kept, taps):
-        acc = jnp.dot(
-            wt[...], jnp.concatenate([tap(h) for tap in taps], axis=0),
+    def own_taps(h):
+        return jnp.dot(
+            wt[...], jnp.concatenate([tap(h) for tap in taps_of_own], axis=0),
             preferred_element_type=F32,
         )
-        even, odd = acc[:, :lanes], acc[:, lanes:]
+
+    def first_frame(h):
+        seen = slab(c)(h)
+        return jnp.dot(
+            wt[...], jnp.concatenate([seen] * 3, axis=0), preferred_element_type=F32
+        )
+
+    def with_z(h):
+        seen = slab(z_slot)(h)
+        return acc[h] + jnp.dot(
+            wz[...], jnp.concatenate([seen] * 2, axis=0), preferred_element_type=F32
+        )
+
+    def conv_row(h, kept, summed):
+        found = summed(h)
+        even, odd = found[:, :lanes], found[:, lanes:]
         before = jnp.where(lane == 0, 0.0, pltpu.roll(odd[0:128], 1, 1))
         after = jnp.where(lane == lanes - 1, 0.0, pltpu.roll(even[256:384], lanes - 1, 1))
         even, odd = (
@@ -254,8 +260,8 @@
         a, b = even.astype(F32), odd.astype(F32)
         return a + b, a * a + b * b
 
-    def conv_rows(places, kept, taps):
-        found = [conv_row(h, kept, taps) for h in places]
+    def conv_rows(places, kept, summed):
+        found = [conv_row(h, kept, summed) for h in places]
         for q in range(2):
             total_q = found[0][q]
             for one in found[1:]:
@@ -279,8 +285,6 @@
                     {"tm": t, "space": s, "chan": c},
                 ).wait_recv()
 
-    gets_z = jnp.logical_or(jnp.logical_and(c == 1, down_ok), jnp.logical_and(c == 0, up_ok))
-
     def wait_z(p):
         @pl.when(gets_z)
         def _():
@@ -301,14 +305,6 @@
             def _(low=low):
                 forward(low).wait_recv()
 
-    row8 = lax.broadcasted_iota(jnp.int32, (8, 128), 0)
-    lane8 = lax.broadcasted_iota(jnp.int32, (8, 128), 1)
-    facts = jnp.where(row8 == 2, jnp.where(has_main, my_clip, -1).astype(F32), -1.0)
-    facts = jnp.where(
-        jnp.logical_and(row8 == 5, first), clip_in[0, 0].astype(F32), facts
-    )
-    stat[...] = facts
-
     half_index = jnp.where(flip, c, 1 - c) if mirror else c
 
     if not mirror:
@@ -324,17 +320,62 @@
                 wait_edges()
         begin = jnp.where(c == 0, half_rows, 0) if mirror else c * half_rows
         conv_rows(
-            [row_of(begin + p) for p in range(half_rows - 1, -1, -1)], 1, [slab(c)] * 3
+            [row_of(begin + p) for p in range(half_rows - 1, -1, -1)], 1, first_frame
         )
         sums_to(3)
 
-    def tap_old(h):
-        return jnp.where(older, slab(0)(h), tap_mid(h))
-
-    def tap_mid(h):
-        return jnp.where(newer, slab(1)(h), slab(2)(h))
-
-    taps = [tap_old, tap_mid, slab(2)]
+    @pl.when(gets_z)
+    def _():
+        meta_copy.wait_recv()
+
+    to_scalars = pltpu.make_async_copy(near_meta, near_ids, local_sem.at[7])
+    to_scalars.start()
+    to_scalars.wait()
+
+    my_clip = jnp.where(c == 1, clip_in[0, 1], near_ids[0, 0])
+    newer = jnp.where(c == 1, clip_in[0, 0], clip_in[0, 1]) == my_clip
+    older = jnp.logical_and(
+        jnp.logical_or(c == 0, t > 0),
+        jnp.where(c == 1, near_ids[0, 1], clip_in[0, 0]) == my_clip,
+    )
+
+    w_old, w_mid, w_new = (
+        wt[:, pl.ds(k * 3 * CHANNELS, 3 * CHANNELS)].astype(F32) for k in range(3)
+    )
+    on_z = jnp.where(
+        c == 0, w_new + jnp.where(newer, 0.0, w_mid + w_old), jnp.where(older, w_old, 0.0)
+    )
+    coarse = on_z.astype(BF16)
+    wz[:, pl.ds(0, 3 * CHANNELS)] = coarse
+    wz[:, pl.ds(3 * CHANNELS, 3 * CHANNELS)] = (on_z - coarse.astype(F32)).astype(BF16)
+
+    row8 = lax.broadcasted_iota(jnp.int32, (8, 128), 0)
+    lane8 = lax.broadcasted_iota(jnp.int32, (8, 128), 1)
+    facts = jnp.where(row8 == 2, jnp.where(has_main, my_clip, -1).astype(F32), -1.0)
+    facts = jnp.where(
+        jnp.logical_and(row8 == 5, first), clip_in[0, 0].astype(F32), facts
+    )
+    stat[pl.ds(2, 1), :] = facts[2:3]
+    stat[pl.ds(5, 1), :] = facts[5:6]
+
+    none = jnp.zeros((3 * CHANNELS, columns), BF16)
+
+    def newest(h):
+        return jnp.where(c == 1, slab(1 + c)(h), none)
+
+    def middle(h):
+        return jnp.where(newer, slab(1)(h), newest(h))
+
+    def oldest(h):
+        return jnp.where(older, jnp.where(c == 0, slab(c)(h), none), middle(h))
+
+    taps_of_own = [oldest, middle, newest]
+
+    def own_rows_of(places):
+        for p in places:
+            h = row_of(p)
+            acc[h] = own_taps(h)
+
     steps = rows // 2
 
     def send_owners():
@@ -353,16 +394,32 @@
         )
         copy.wait_recv() if received else copy.wait_send()
 
+    tail = (rows - 3, 0, rows - 2, rows - 1)
+
+    @pl.when(has_main)
+    def _():
+        own_rows_of(range(1, rows - 3))
+
     if mirror:
         wait_z(0)
         start_forwards()
-        wait_z(1)
+
+        @pl.when(jnp.logical_not(jnp.logical_and(first, c == 1)))
+        def _():
+            wait_edges()
     else:
         for p in range(rows):
             wait_z(p)
         start_forwards()
         wait_forwards()
 
+    @pl.when(has_main)
+    def _():
+        own_rows_of(tail)
+
+    if mirror:
+        wait_z(1)
+
     sums[...] = jnp.zeros_like(sums)
 
     @pl.loop(0, steps - 2)
@@ -373,19 +430,16 @@
 
         @pl.when(has_main)
         def _():
-            conv_rows([row_of(2 * n + 1), row_of(2 * n + 2)], 0, taps)
+            conv_rows([row_of(2 * n + 1), row_of(2 * n + 2)], 0, with_z)
 
     if mirror:
-        @pl.when(jnp.logical_not(jnp.logical_and(first, c == 1)))
-        def _():
-            wait_edges()
         wait_z(rows - 2)
         wait_forwards()
         wait_z(rows - 1)
 
     @pl.when(has_main)
     def _():
-        conv_rows([row_of(p) for p in (rows - 3, 0, rows - 2, rows - 1)], 0, taps)
+        conv_rows([row_of(p) for p in tail], 0, with_z)
 
     @pl.when(has_main)
     def _():
@@ -583,7 +637,6 @@
         @pl.when(ok)
         def _(up=up):
             z_copy(up, 0, rows).wait_send()
-            meta_copy(up).wait_send()
     for low, ok in sides:
         @pl.when(ok)
         def _(low=low):
@@ -596,6 +649,10 @@
             @pl.when(gets_z)
             def _():
                 forward(low).wait_send()
+
+    @pl.when(meta_sent)
+    def _():
+        meta_copy.wait_send()
 
     stat_wait(False)
     owner_wait(False)
@@ -641,11 +698,13 @@
                 pltpu.VMEM((1, CHANNELS), F32),
                 pltpu.VMEM((4, moments, CHANNELS), BF16),
                 pltpu.VMEM((8, 128), jnp.int32),
-                pltpu.VMEM((2, 8, 128), jnp.int32),
-                pltpu.SMEM((2, 8, 128), jnp.int32),
+                pltpu.VMEM((8, 128), jnp.int32),
+                pltpu.SMEM((8, 128), jnp.int32),
                 pltpu.VMEM((n_tm, 8, 128), jnp.int32),
                 pltpu.VMEM((3, rows + 2, 2, half, columns), BF16),
                 pltpu.VMEM((384, 1152), BF16),
+                pltpu.VMEM((384, 768), BF16),
+                pltpu.VMEM((rows, 384, columns), F32),
                 pltpu.VMEM((2, rows, CHANNELS, columns), BF16),
                 pltpu.VMEM((8, 128), F32),
                 pltpu.VMEM((total, 8, 128), F32),

time: 22.8 us -> 22.3 us (0.978)
  Pallas kernels: 22 us -> 21.5 us
    pallas_call x1, Pallas kernels: 22 us -> 21.5 us  [shards(): pl.pallas_call(functools.partial(kernel, (n_tm, n_space, capacity)), out_...]
where the time goes in v5:
time: 22.3 us; the launch traced here: 22.1 us
  Pallas kernels  21.5 us (96%)
  local copies, waits for them, and re-layouts  0.63 us (3%)
    pallas_call x1, Pallas kernels, shards(): pl.pallas_call(functools.partial(kernel, (n_tm, n_space, capacity)), out_...  21.5 us
    unnamed x1, local copies, waits for them, and re-layouts  0.63 us

profile of v5, /device:TPU:0, one launch (start us, length us, event | category | flops | bytes accessed | tf_op | source)
XLA Modules:
  0.0 22.1 jit_solution(6557365109769038206)
XLA Ops:
  0.0 21.5 %shard_map.73 = bf16[1,16,16,128]{3,2,1,0:T(8,128)(2,1)S(1)} custom-call(s32[1,2]{1,0:T(1,128)} %bitcast.8, s32[1,8]{1,0:T(1,128)} %bitcast.9, bf16[64,2,8,256]{3,2,1,0:T(8,128)(2,1)} %act_in.1, bf16[3,3,3,128,128]{4,3,2,1,0:T(8,128)(2,1)} %weight_in.1, f32[1,128]{1,0:T(1,128)} %bitcast.10, f32[1,128]{1,0:T(1,128)} %bitcast.11, bf16[4,32,128]{2,1,0:T(8,128)(2,1)} %bitcast.7), custom_call_target="tpu_custom_call" | custom-call | tf_op jit(solution)/shard_map/pallas_call | solution.py:685
  21.5 0.6 %copy.9 = bf16[1,16,16,128]{3,2,1,0:T(8,128)(2,1)} copy(bf16[1,16,16,128]{3,2,1,0:T(8,128)(2,1)S(1)} %shard_map.73) | data formatting | bytes 131072

commit v6 on v5

--- a/solution.py
+++ b/solution.py
@@ -143,12 +143,15 @@
             device_id_type=MESH,
         )
 
-    def z_copy(up, p, count):
+    groups = ((0, 1), (1, rows - 3), (rows - 2, 2))
+
+    def z_copy(up, group):
+        p, count = groups[group]
         frame, slot, core, tt = (1, 0, 1, t_up) if up else (0, 2, 0, t_down)
         begin = 1 + (jnp.where(flip, rows - p - count, p) if mirror else p)
         return remote(
             x.at[c + frame, pl.ds(begin, count), c], x.at[slot, pl.ds(begin, count), c],
-            z_send.at[int(up)], z_recv.at[p], {"tm": tt, "space": s, "chan": core},
+            z_send.at[int(up)], z_recv.at[group], {"tm": tt, "space": s, "chan": core},
         )
 
     meta_copy = remote(
@@ -183,11 +186,11 @@
     zs = ((True, up_ok), (False, down_ok))
     sides = ((True, low_ok), (False, high_ok))
 
-    def start_z(p):
+    def start_z(group):
         for up, ok in zs:
             @pl.when(ok)
             def _(up=up):
-                z_copy(up, p, 1).start()
+                z_copy(up, group).start()
 
     @pl.when(meta_sent)
     def _():
@@ -195,14 +198,13 @@
 
     peer.start()
     start_z(0)
-    start_z(1)
     for low, ok in sides:
         @pl.when(ok)
         def _(low=low):
             edge(low, 0).start()
             edge(low, 1).start()
-    for p in range(2, rows):
-        start_z(p)
+    start_z(1)
+    start_z(2)
 
     if rounds > 0:
         greet(round_sem.at[0])
@@ -243,9 +245,7 @@
 
     def with_z(h):
         seen = slab(z_slot)(h)
-        return acc[h] + jnp.dot(
-            wz[...], jnp.concatenate([seen] * 2, axis=0), preferred_element_type=F32
-        )
+        return acc[h] + jnp.dot(wz[...], seen, preferred_element_type=F32)
 
     def conv_row(h, kept, summed):
         found = summed(h)
@@ -285,12 +285,15 @@
                     {"tm": t, "space": s, "chan": c},
                 ).wait_recv()
 
-    def wait_z(p):
+    def wait_z(group):
+        p, count = groups[group]
+
         @pl.when(gets_z)
         def _():
-            there = x.at[z_slot, pl.ds(1 + row_of(p), 1)]
+            begin = 1 + (jnp.where(flip, rows - p - count, p) if mirror else p)
+            there = x.at[z_slot, pl.ds(begin, count)]
             remote(
-                there, there, z_send.at[0], z_recv.at[p], {"tm": t, "space": s, "chan": c}
+                there, there, z_send.at[0], z_recv.at[group], {"tm": t, "space": s, "chan": c}
             ).wait_recv()
 
     def start_forwards():
@@ -345,9 +348,7 @@
     on_z = jnp.where(
         c == 0, w_new + jnp.where(newer, 0.0, w_mid + w_old), jnp.where(older, w_old, 0.0)
     )
-    coarse = on_z.astype(BF16)
-    wz[:, pl.ds(0, 3 * CHANNELS)] = coarse
-    wz[:, pl.ds(3 * CHANNELS, 3 * CHANNELS)] = (on_z - coarse.astype(F32)).astype(BF16)
+    wz[...] = on_z.astype(BF16)
 
     row8 = lax.broadcasted_iota(jnp.int32, (8, 128), 0)
     lane8 = lax.broadcasted_iota(jnp.int32, (8, 128), 1)
@@ -408,8 +409,8 @@
         def _():
             wait_edges()
     else:
-        for p in range(rows):
-            wait_z(p)
+        for group in range(3):
+            wait_z(group)
         start_forwards()
         wait_forwards()
 
@@ -417,25 +418,18 @@
     def _():
         own_rows_of(tail)
 
+    sums[...] = jnp.zeros_like(sums)
+
     if mirror:
         wait_z(1)
 
-    sums[...] = jnp.zeros_like(sums)
-
-    @pl.loop(0, steps - 2)
-    def _(n):
-        if mirror:
-            wait_z(2 * n + 2)
-            wait_z(2 * n + 3)
-
-        @pl.when(has_main)
-        def _():
-            conv_rows([row_of(2 * n + 1), row_of(2 * n + 2)], 0, with_z)
+    @pl.when(has_main)
+    def _():
+        conv_rows([row_of(p) for p in range(1, rows - 3)], 0, with_z)
 
     if mirror:
-        wait_z(rows - 2)
         wait_forwards()
-        wait_z(rows - 1)
+        wait_z(2)
 
     @pl.when(has_main)
     def _():
@@ -636,7 +630,11 @@
     for up, ok in zs:
         @pl.when(ok)
         def _(up=up):
-            z_copy(up, 0, rows).wait_send()
+            span = x.at[0, pl.ds(1, rows), 0]
+            remote(
+                span, span, z_send.at[int(up)], z_recv.at[0],
+                {"tm": t, "space": s, "chan": c},
+            ).wait_send()
     for low, ok in sides:
         @pl.when(ok)
         def _(low=low):
@@ -703,7 +701,7 @@
                 pltpu.VMEM((n_tm, 8, 128), jnp.int32),
                 pltpu.VMEM((3, rows + 2, 2, half, columns), BF16),
                 pltpu.VMEM((384, 1152), BF16),
-                pltpu.VMEM((384, 768), BF16),
+                pltpu.VMEM((384, 384), BF16),
                 pltpu.VMEM((rows, 384, columns), F32),
                 pltpu.VMEM((2, rows, CHANNELS, columns), BF16),
                 pltpu.VMEM((8, 128), F32),
@@ -714,7 +712,7 @@
                 pltpu.VMEM((2, CHANNELS, columns // 2), F32),
                 pltpu.SemaphoreType.REGULAR((2,)),
                 dma((2,)),
-                dma((rows,)),
+                dma((3,)),
                 dma((2,)),
                 dma((2,)),
                 dma((2,)),

time: 22.3 us -> 21.7 us (0.973)
  Pallas kernels: 21.5 us -> 20.9 us
    pallas_call x1, Pallas kernels: 21.5 us -> 20.9 us  [shards(): pl.pallas_call(functools.partial(kernel, (n_tm, n_space, capacity)), out_...]
where the time goes in v6:
time: 21.7 us; the launch traced here: 21.5 us
  Pallas kernels  20.9 us (96%)
  local copies, waits for them, and re-layouts  0.63 us (3%)
    pallas_call x1, Pallas kernels, shards(): pl.pallas_call(functools.partial(kernel, (n_tm, n_space, capacity)), out_...  20.9 us
    unnamed x1, local copies, waits for them, and re-layouts  0.63 us

profile of v6, /device:TPU:0, one launch (start us, length us, event | category | flops | bytes accessed | tf_op | source)
XLA Modules:
  0.0 21.5 jit_solution(12106315261895837324)
XLA Ops:
  0.0 20.9 %shard_map.73 = bf16[1,16,16,128]{3,2,1,0:T(8,128)(2,1)S(1)} custom-call(s32[1,2]{1,0:T(1,128)} %bitcast.8, s32[1,8]{1,0:T(1,128)} %bitcast.9, bf16[64,2,8,256]{3,2,1,0:T(8,128)(2,1)} %act_in.1, bf16[3,3,3,128,128]{4,3,2,1,0:T(8,128)(2,1)} %weight_in.1, f32[1,128]{1,0:T(1,128)} %bitcast.10, f32[1,128]{1,0:T(1,128)} %bitcast.11, bf16[4,32,128]{2,1,0:T(8,128)(2,1)} %bitcast.7), custom_call_target="tpu_custom_call" | custom-call | tf_op jit(solution)/shard_map/pallas_call | solution.py:683
  20.9 0.6 %copy.9 = bf16[1,16,16,128]{3,2,1,0:T(8,128)(2,1)} copy(bf16[1,16,16,128]{3,2,1,0:T(8,128)(2,1)S(1)} %shard_map.73) | data formatting | bytes 131072

commit v7 on v6

--- a/solution.py
+++ b/solution.py
@@ -592,39 +592,49 @@
     owners.start()
     owners.wait()
 
-    def arrived_wait(count):
-        span = arrived.at[pl.ds(0, count)]
-        remote(
-            span, span, lat_send.at[0], lat_recv.at[0], {"tm": t, "space": s, "chan": c}
-        ).wait_recv()
-
-    every = n_frames * lat_rows
-
-    @pl.when(first)
-    def _():
-        arrived_wait(every - lat_rows - piece_rows)
-
-    @pl.when(jnp.logical_and(has_main, t > 0))
-    def _():
-        arrived_wait(every - lat_rows)
-
-    @pl.when(jnp.logical_not(has_main))
-    def _():
-        arrived_wait(every)
-
-    @pl.loop(0, n_tm)
-    def _(b):
+    def slots_of(b):
         taken = jnp.int32(0)
         slots = []
         for n in range(own_rows):
             hit = ids[b, 0, frames_here + n] == t
             slots.append(jnp.where(hit, taken, -1))
             taken = taken + jnp.where(hit, 1, 0)
+        return slots
+
+    def place(b, slots):
         for j in range(capacity):
             value = jnp.zeros((16, lanes), BF16)
             for n in range(own_rows):
                 value = jnp.where(slots[n] == j, arrived[b * own_rows + n], value)
             out[0, b * capacity + j] = value
+
+    known = [slots_of(b) for b in range(n_tm)] if n_tm <= 4 else None
+
+    def arrived_wait(count):
+        span = arrived.at[pl.ds(0, count)]
+        remote(
+            span, span, lat_send.at[0], lat_recv.at[0], {"tm": t, "space": s, "chan": c}
+        ).wait_recv()
+
+    every = n_frames * lat_rows
+
+    @pl.when(first)
+    def _():
+        arrived_wait(every - lat_rows - piece_rows)
+
+    @pl.when(jnp.logical_and(has_main, t > 0))
+    def _():
+        arrived_wait(every - lat_rows)
+
+    @pl.when(jnp.logical_not(has_main))
+    def _():
+        arrived_wait(every)
+
+    if known is None:
+        pl.loop(0, n_tm)(lambda b: place(b, slots_of(b)))
+    else:
+        for b in range(n_tm):
+            place(b, known[b])
 
     peer.wait_send()
     for up, ok in zs:

time: 21.7 us -> 21.7 us (level)
  no operation moved by 1% of the time
where the time goes in v7:
time: 21.7 us; the launch traced here: 21.4 us
  Pallas kernels  20.8 us (96%)
  local copies, waits for them, and re-layouts  0.63 us (3%)
    pallas_call x1, Pallas kernels, shards(): pl.pallas_call(functools.partial(kernel, (n_tm, n_space, capacity)), out_...  20.8 us
    unnamed x1, local copies, waits for them, and re-layouts  0.63 us

profile of v7, /device:TPU:0, one launch (start us, length us, event | category | flops | bytes accessed | tf_op | source)
XLA Modules:
  0.0 21.4 jit_solution(2192364387975312995)
XLA Ops:
  0.0 20.8 %shard_map.73 = bf16[1,16,16,128]{3,2,1,0:T(8,128)(2,1)S(1)} custom-call(s32[1,2]{1,0:T(1,128)} %bitcast.8, s32[1,8]{1,0:T(1,128)} %bitcast.9, bf16[64,2,8,256]{3,2,1,0:T(8,128)(2,1)} %act_in.1, bf16[3,3,3,128,128]{4,3,2,1,0:T(8,128)(2,1)} %weight_in.1, f32[1,128]{1,0:T(1,128)} %bitcast.10, f32[1,128]{1,0:T(1,128)} %bitcast.11, bf16[4,32,128]{2,1,0:T(8,128)(2,1)} %bitcast.7), custom_call_target="tpu_custom_call" | custom-call | tf_op jit(solution)/shard_map/pallas_call | solution.py:693
  20.8 0.6 %copy.9 = bf16[1,16,16,128]{3,2,1,0:T(8,128)(2,1)} copy(bf16[1,16,16,128]{3,2,1,0:T(8,128)(2,1)S(1)} %shard_map.73) | data formatting | bytes 131072
